TPU v7x, 512 devices: a whole 4x8x8 slice. The times are simulated.
512 devices in a mesh: tp: 16 (over x_hi, y), grp: 32 (over x_lo, z, core).
Axes of the slice: x: 4 (x_hi: 2, x_lo: 2; x = x_hi * 2 + x_lo), y: 8, z: 8, core: 2. Of those that a mesh axis runs over, the one named last changes fastest.
Arguments:
- low_feats: bfloat16 [1536, 16384], P('grp', 'tp'), may hold values from -40 to 40
- mid_feats: bfloat16 [1536, 16384], P('grp', 'tp'), may hold values from -40 to 40
- high_feats: bfloat16 [1536, 16384], P('grp', 'tp'), may hold values from -40 to 40
- w_low: bfloat16 [16384, 16384], P('tp', 'grp'), may hold values from -3 to 3
- w_mid: bfloat16 [16384, 16384], P('tp', 'grp'), may hold values from -3 to 3
- w_high: bfloat16 [16384, 16384], P('tp', 'grp'), may hold values from -3 to 3
- norm_gain: float32 [16384], P('grp'), may hold values from 0.1 to 1.9
- accepted: int32 [256], replicated, may hold values from 0 to 5, as said below
- assignment: int32 [256], replicated, may hold values from 0 to 255, each once
Outputs:
- drafted: bfloat16 [1536, 16384], P('tp', 'grp')
Inputs may be any that keep to these rules, and one draw needn't show every extreme that they name: For every group of 8 consecutive rows starting at a multiple of 8, the sum of accepted + 1 is at most 32, and some group reaches 32; rows 2i and 2i+1 together have at most 8 positions with p <= accepted. `assignment`: each row appears once.
All inputs are finite; a program needn't handle non-finite values.
Results may differ from a plain program's by a relative error of at most 0.0008.
Values may be sent and summed in bfloat16 or wider, within the bound.
No kernel may reach another device: no remote copies, remote signals or barrier semaphores. Data moves between devices by JAX's collectives and lax.ppermute only.
A program may use at most 64 MiB of HBM per device.

v0:
```python
import jax
import jax.numpy as jnp
from jax import lax
from jax.experimental import pallas as pl
from jax.experimental.pallas import tpu as pltpu
from jax.sharding import Mesh
from jax.sharding import PartitionSpec as P

D = 16384
ROWS_G = 8
POS = 6
SLOTS = 8
EPSILON = 1e-05
TP = ("xh", "y")
GRP = ("xl", "z", "c")
SWAP = [(0, 1), (1, 0)]


def both_ways(n):
    pairs = []
    for i in range(n):
        for c in range(2):
            to = (i + (1 if c == 0 else n - 1)) % n
            pairs.append((i * 2 + c, to * 2 + c))
    return pairs


def diagonal(n):
    pairs = []
    for x in range(2):
        for i in range(n):
            for c in range(2):
                to = (i + (1 if c == 0 else n - 1)) % n
                pairs.append(((x * n + i) * 2 + c, ((1 - x) * n + to) * 2 + c))
    return pairs


def other_core(x):
    return lax.ppermute(x, "c", SWAP)


def onward(x, axis):
    return lax.ppermute(x, (axis, "c"), both_ways(lax.axis_size(axis)))


VMEM = pl.BlockSpec(memory_space=pltpu.VMEM)
SMEM = pl.BlockSpec(memory_space=pltpu.SMEM)
SMALL = pltpu.CompilerParams(vmem_limit_bytes=8 << 20)


def joined(*parts):
    def kernel(*refs):
        at = 0
        for ref in refs[:-1]:
            refs[-1][at : at + ref.shape[0]] = ref[...]
            at += ref.shape[0]

    shape = (sum(p.shape[0] for p in parts), *parts[0].shape[1:])
    return pl.pallas_call(
        kernel,
        out_shape=jax.ShapeDtypeStruct(shape, parts[0].dtype),
        in_specs=[VMEM] * len(parts),
        out_specs=VMEM,
        compiler_params=SMALL,
        name="joined",
    )(*parts)


def each_row(me, first, turn, values, block, do):
    xh, y, c, ny = me[0], me[1], me[2], 8
    k, v = block // 2 - 4, block % 2
    if k == -4:
        h = jnp.where(c == v, 1 - xh, xh)
    else:
        h = xh if v else 1 - xh
    slab = h * ny + lax.rem(y + (1 - 2 * c) * k + ny, ny)
    per_slab = first.shape[0] // (2 * ny)

    @pl.loop(0, per_slab)
    def _(i):
        start, by = first[slab * per_slab + i], turn[slab * per_slab + i]
        for p in range(POS):
            do(i * POS + p, values[pl.ds(start + by * p, 1), :])


def taken(table, blocks):
    _, first, _, values = table

    def kernel(me, first, turn, values, out):
        for n, block in enumerate(blocks):

            def store(r, row, n=n):
                out[n, pl.ds(r, 1), :] = row

            each_row(me, first, turn, values, block, store)

    return pl.pallas_call(
        kernel,
        out_shape=jax.ShapeDtypeStruct(
            (len(blocks), first.shape[0] // 16 * POS, values.shape[1]), values.dtype
        ),
        in_specs=[SMEM, SMEM, SMEM, VMEM],
        out_specs=VMEM,
        compiler_params=SMALL,
        name="taken",
    )(*table)


def paired(table, block, theirs, at, came=None, first_step=False):
    def kernel(*refs):
        me, first, turn, values, theirs = refs[:5]
        out = refs[-1]

        def store(r, row):
            out[0, pl.ds(r, 1), :] = row

        each_row(me, first, turn, values, block, store)
        if came is None:
            out[1] = theirs[at]
        elif not first_step:
            out[0] = out[0] + refs[5][0]
            out[1] = theirs[at] + refs[5][1]
        else:
            wanted = me[2] == block % 2
            out[0] = out[0] + jnp.where(wanted, refs[5][0], 0.0)
            out[1] = theirs[at] + jnp.where(wanted, refs[5][1], 0.0)

    more = [] if came is None else [came]
    return pl.pallas_call(
        kernel,
        out_shape=jax.ShapeDtypeStruct((2, *theirs.shape[1:]), theirs.dtype),
        in_specs=[SMEM, SMEM, SMEM, VMEM, VMEM, VMEM][: 5 + len(more)],
        out_specs=VMEM,
        compiler_params=SMALL,
        name="paired",
    )(*table, theirs, *more)


def pick_kernel(group, accepted, low, mid, high, out, used_by, held, sems):
    feats = (low, mid, high)
    copies = [pltpu.make_async_copy(accepted, used_by, sems.at[3])]
    copies += [pltpu.make_async_copy(f, held.at[i], sems.at[i]) for i, f in enumerate(feats)]
    for copy in copies:
        copy.start()
    slots, (tokens, k) = out.shape[0], low.shape
    slot = lax.broadcasted_iota(jnp.int32, (slots, tokens), 0)
    token = lax.broadcasted_iota(jnp.int32, (slots, tokens), 1)
    pair, at = slot // SLOTS, slot % SLOTS
    used = jnp.zeros_like(slot)
    copies[0].wait()
    for i in range(ROWS_G // 2):
        used = jnp.where(pair == i, used_by[group[0] * ROWS_G + 2 * i] + 1, used)
    source = pair * (2 * POS) + jnp.where(at < used, at, 2 * POS + 1 - at)
    pick = jnp.where(source == token, 1.0, 0.0).astype(jnp.bfloat16)
    for i in range(3):
        copies[1 + i].wait()
        out[:, i * k : (i + 1) * k] = jnp.dot(
            pick, held[i], preferred_element_type=jnp.float32
        ).astype(jnp.bfloat16)


def selected(feats, group, accepted):
    slots, width = ROWS_G // 2 * SLOTS, 3 * feats[0].shape[1]
    return pl.pallas_call(
        pick_kernel,
        out_shape=jax.ShapeDtypeStruct((slots, width), jnp.bfloat16),
        in_specs=[SMEM] + [pl.BlockSpec(memory_space=pl.ANY)] * 4,
        out_specs=VMEM,
        scratch_shapes=[
            pltpu.SMEM(accepted.shape, jnp.int32),
            pltpu.VMEM((3, *feats[0].shape), jnp.bfloat16),
            pltpu.SemaphoreType.DMA((4,)),
        ],
        compiler_params=pltpu.CompilerParams(vmem_limit_bytes=60 << 20),
        name="pick",
    )(group[None], accepted, *feats)


def product(parts, weights, rows, at, before=None):
    k, columns = weights[0].shape
    count = sum(n for _, _, n in parts)

    arrays = []
    for p, _, _ in parts:
        if not any(p is q for q in arrays):
            arrays.append(p)
    which = [next(i for i, q in enumerate(arrays) if q is p) for p, _, _ in parts]

    def kernel(*refs):
        n = len(arrays)
        ws, out, held = refs[n : n + 3], refs[-2], refs[-1]
        to = 0
        for i, (_, start, number) in zip(which, parts, strict=True):
            held[to : to + number] = refs[i][start : start + number]
            to += number
        total = jnp.dot(held[:, :k], ws[0][...], preferred_element_type=jnp.float32)
        for i in (1, 2):
            total += jnp.dot(
                held[:, i * k : (i + 1) * k], ws[i][...], preferred_element_type=jnp.float32
            )
        out[at : at + count] = total

    operands = arrays + list(weights)
    aliases = {} if before is None else {len(operands): 0}
    return pl.pallas_call(
        kernel,
        out_shape=jax.ShapeDtypeStruct((rows, columns), jnp.float32),
        in_specs=[VMEM] * (len(operands) + len(aliases)),
        out_specs=VMEM,
        scratch_shapes=[pltpu.VMEM((count, 3 * k), jnp.bfloat16)],
        input_output_aliases=aliases,
        compiler_params=pltpu.CompilerParams(vmem_limit_bytes=12 << 20),
        name="product",
    )(*operands, *([] if before is None else [before]))


def step_on_device(
    low_feats, mid_feats, high_feats, w_low, w_mid, w_high, norm_gain, accepted, assignment
):
    weights = (w_low, w_mid, w_high)
    xh, y, xl, z, c = (lax.axis_index(a) for a in ("xh", "y", "xl", "z", "c"))
    ny, nz = lax.axis_size("y"), lax.axis_size("z")
    way = 1 - 2 * c
    group = (xl * nz + z) * 2 + c
    mine = selected((low_feats, mid_feats, high_feats), group, accepted)
    block = mine.shape[0]

    chip = joined(mine, other_core(mine))
    straight = [onward(chip, "z")]
    crossed = [lax.ppermute(chip, GRP, diagonal(nz))]
    beside = lax.ppermute(mine, "xl", SWAP)
    for _ in range(2):
        straight.append(onward(straight[-1], "z"))
        crossed.append(onward(crossed[-1], "z"))
    straight.append(onward(straight[-1][:block], "z"))
    crossed.append(onward(crossed[-1][:block], "z"))
    here, there = [], []
    for s in range(4):
        here.append(joined(straight[s], crossed[s], *((beside,) if s == 1 else ())))
        there.append(other_core(here[s]))
    cut = 4 * block
    total = 32 * block
    partial_value = product([(chip, 0, 2 * block)], weights, total, 0)
    parts = [
        (beside, 0, block),
        (there[1], cut, block),
        (here[0], 0, cut),
        (there[0], 0, cut),
        (here[1], 0, cut),
        (there[1], 0, cut),
    ]
    partial_value = product(parts, weights, total, 2 * block, partial_value)
    parts = [
        (here[2], 0, cut),
        (there[2], 0, cut),
        (here[3], 0, 2 * block),
        (there[3], 0, 2 * block),
    ]
    partial_value = product(parts, weights, total, 20 * block, partial_value)

    per_slab = assignment.shape[0] // (2 * ny)
    target = assignment
    of_group = target // ROWS_G
    there_c, there_z, there_x = of_group % 2, (of_group // 2) % nz, of_group // (2 * nz)
    dx, dc, dz = there_x ^ xl, there_c ^ c, (there_z - z) % nz
    step = (-way * dz) % nz
    near = jnp.minimum(step, nz - step)
    from_here = step < nz // 2
    place = jnp.where(
        near == 0,
        dx * 2 + dc,
        jnp.where(
            near == nz // 2,
            28 + dc * 2 + dx,
            near * 8 - 4 + jnp.where(from_here, dx * 2 + dc, 5 + dx * 2 - dc),
        ),
    )
    in_group = target % ROWS_G
    even = in_group % 2 == 0
    first = place * block + (in_group // 2) * SLOTS + jnp.where(even, 0, SLOTS - 1)
    turn = jnp.where(even, 1, -1)
    size = per_slab * POS

    table = (jnp.stack([xh, y, c]), first, turn, partial_value)
    far = taken(table, (1,))
    behind = taken(table, tuple(range(2, 8)))
    beyond = taken(table, (8,))[0]
    own = taken(table, (9,))[0]
    far = paired(table, 0, other_core(far), 0)
    far = onward(far, "y")
    behind = other_core(behind)
    across = lax.ppermute(beyond, "xh", SWAP)
    came = [far, far]
    for step, k in enumerate((3, 2, 1)):
        for v in range(2):
            total = paired(
                table, 8 + 2 * k + v, behind, 2 * step + v, came[v], step == 0
            )
            if k == 1 and v == 0:
                came[v] = lax.ppermute(total, (*TP, "c"), diagonal(ny))
            else:
                came[v] = onward(total, "y")
    given = other_core(came[0][1] + came[1][1])
    summed = own + across + came[0][0] + came[1][0] + given

    squares = jnp.sum(summed * summed, axis=1)
    squares = jnp.sum(
        lax.all_to_all(
            jnp.broadcast_to(squares[None], (4 * nz, size)), GRP, 0, 0, tiled=True
        ),
        axis=0,
    )
    inverse = lax.rsqrt(squares / D + EPSILON)
    own_target = lax.dynamic_slice(target, ((xh * ny + y) * per_slab,), (per_slab,))
    own_used = jnp.sum(
        jnp.where(
            own_target[:, None] == jnp.arange(accepted.shape[0], dtype=jnp.int32)[None, :],
            accepted[None, :],
            0,
        ),
        axis=1,
    )
    live = (jnp.arange(POS, dtype=jnp.int32)[None, :] <= own_used[:, None]).reshape(size)
    normed = summed * inverse[:, None] * norm_gain[None, :]
    return jnp.where(live[:, None], normed, jnp.zeros_like(normed)).astype(jnp.bfloat16)


def solution(mesh):
    split = Mesh(mesh.devices.reshape(2, 8, 2, 8, 2), ("xh", "y", "xl", "z", "c"))
    feats, weight = P(GRP, TP), P(TP, GRP)
    return jax.shard_map(
        step_on_device,
        mesh=split,
        in_specs=(feats, feats, feats, weight, weight, weight, P(GRP), P(), P()),
        out_specs=P(TP, GRP),
        check_vma=False,
    )
```

profile of v0, /device:TPU:1, one launch (start us, length us, event | category | flops | bytes accessed | tf_op | source)
XLA Modules:
  0.0 162.9 jit_solution(16376474730033649256)
XLA Ops:
  0.0 2.0 %pick.1.refs_0_ = bf16[32,3072]{1,0:T(8,128)(2,1)} custom-call(s32[1]{0:T(128)} %bitcast.3.group, s32[256]{0:T(256)} %accepted.1, bf16[48,1024]{1,0:T(8,128)(2,1)} %low.1, bf16[48,1024]{1,0:T(8,128)(2,1)} %mid.1, bf16[48,1024]{1,0:T(8,128)(2,1)} %high.1), custom_call_target="tpu_custom_call" | custom-call | tf_op jit(solution)/shard_map/pick/pallas_call | solution.py:164
  2.0 8.8 %collective-permute-start = (bf16[32,3072]{1,0:T(8,128)(2,1)}, bf16[32,3072]{1,0:T(8,128)(2,1)S(1)}, u32[]{:S(2)}, u32[]{:S(2)}) collective-permute-start(bf16[32,3072]{1,0:T(8,128)(2,1)} %pick.1.refs_0_), channel_id=1, source_target_pairs={{0,1},{1,0},{2,3},{3,2},{4,5},{5,4},{6,7},{7,6},{8,9},{9,8},{10,11... | collective-permute-start | bytes 589832 | tf_op jit(solution)/shard_map/ppermute | solution.py:39
  10.8 1.3 collective-permute-done.refs_1_
  12.1 0.9 copy-done.5
  13.0 5.3 %collective-permute-start.1 = (bf16[64,3072]{1,0:T(8,128)(2,1)S(1)}, bf16[64,3072]{1,0:T(8,128)(2,1)S(1)}, u32[]{:S(2)}, u32[]{:S(2)}) collective-permute-start(bf16[64,3072]{1,0:T(8,128)(2,1)S(1)} %joined.5.refs_0_), channel_id=1, source_target_pairs={{0,2},{1,15},{2,4},{3,1},{4,6},{5,3},{6,8},{7,5},{8,10},{9,7},{10,... | collective-permute-start | bytes 1179656 | tf_op jit(solution)/shard_map/ppermute | solution.py:43
  18.3 3.1 %collective-permute-start.4 = (bf16[64,3072]{1,0:T(8,128)(2,1)S(1)}, bf16[64,3072]{1,0:T(8,128)(2,1)S(1)}, u32[]{:S(2)}, u32[]{:S(2)}) collective-permute-start(bf16[64,3072]{1,0:T(8,128)(2,1)S(1)} %joined.5.refs_0_), channel_id=1, source_target_pairs={{0,18},{1,31},{2,20},{3,17},{4,22},{5,19},{6,24},{7,21},{8,26},{9,... | collective-permute-start | bytes 1179656 | tf_op jit(solution)/shard_map/ppermute | solution.py:230
  21.5 1.6 collective-permute-done.1.refs_0_
  23.0 5.0 %collective-permute-start.2 = (bf16[64,3072]{1,0:T(8,128)(2,1)S(1)}, bf16[64,3072]{1,0:T(8,128)(2,1)S(1)}, u32[]{:S(2)}, u32[]{:S(2)}) collective-permute-start(bf16[64,3072]{1,0:T(8,128)(2,1)S(1)} %collective-permute-done.1.refs_0_), channel_id=1, source_target_pairs={{0,2},{1,15},{2,4},{3,1},{4,6},{5,3},{6,8},{7,5},{8,10},{9,7},{10,... | collective-permute-start | bytes 1179656 | tf_op jit(solution)/shard_map/ppermute | solution.py:43
  28.1 3.6 %collective-permute-done.4.refs_1_ = bf16[64,3072]{1,0:T(8,128)(2,1)S(1)} collective-permute-done((bf16[64,3072]{1,0:T(8,128)(2,1)S(1)}, bf16[64,3072]{1,0:T(8,128)(2,1)S(1)}, u32[]{:S(2)}, u32[]{:S(2)}) %collective-permute-start.4) | collective-permute-done | bytes 393248 | tf_op jit(solution)/shard_map/ppermute | solution.py:230
  31.6 4.6 %collective-permute-start.5 = (bf16[64,3072]{1,0:T(8,128)(2,1)S(1)}, bf16[64,3072]{1,0:T(8,128)(2,1)S(1)}, u32[]{:S(2)}, u32[]{:S(2)}) collective-permute-start(bf16[64,3072]{1,0:T(8,128)(2,1)S(1)} %collective-permute-done.4.refs_1_), channel_id=1, source_target_pairs={{0,2},{1,15},{2,4},{3,1},{4,6},{5,3},{6,8},{7,5},{8,10},{9,7},{10,... | collective-permute-start | bytes 1179656 | tf_op jit(solution)/shard_map/ppermute | solution.py:43
  36.2 2.2 %collective-permute-start.11 = (bf16[32,3072]{1,0:T(8,128)(2,1)S(1)}, bf16[32,3072]{1,0:T(8,128)(2,1)S(1)}, u32[]{:S(2)}, u32[]{:S(2)}) collective-permute-start(bf16[32,3072]{1,0:T(8,128)(2,1)S(1)} %copy-done.5), channel_id=1, source_target_pairs={{0,16},{16,0},{1,17},{17,1},{2,18},{18,2},{3,19},{19,3},{4,20},{20... | collective-permute-start | bytes 589832 | tf_op jit(solution)/shard_map/ppermute | solution.py:231
  38.4 1.9 %collective-permute-start.3 = (bf16[64,3072]{1,0:T(8,128)(2,1)S(1)}, bf16[64,3072]{1,0:T(8,128)(2,1)S(1)}, u32[]{:S(2)}, u32[]{:S(2)}) collective-permute-start(bf16[64,3072]{1,0:T(8,128)(2,1)S(1)} %collective-permute-done.2.refs_0_), channel_id=1, source_target_pairs={{0,2},{1,15},{2,4},{3,1},{4,6},{5,3},{6,8},{7,5},{8,10},{9,7},{10,... | collective-permute-start | bytes 1179656 | tf_op jit(solution)/shard_map/ppermute | solution.py:43
  40.3 0.6 collective-permute-done.5.refs_1_
  40.9 5.0 %collective-permute-start.6 = (bf16[64,3072]{1,0:T(8,128)(2,1)S(1)}, bf16[64,3072]{1,0:T(8,128)(2,1)S(1)}, u32[]{:S(2)}, u32[]{:S(2)}) collective-permute-start(bf16[64,3072]{1,0:T(8,128)(2,1)S(1)} %collective-permute-done.5.refs_1_), channel_id=1, source_target_pairs={{0,2},{1,15},{2,4},{3,1},{4,6},{5,3},{6,8},{7,5},{8,10},{9,7},{10,... | collective-permute-start | bytes 1179656 | tf_op jit(solution)/shard_map/ppermute | solution.py:43
  46.0 1.0 joined.8.refs_4_
  47.0 2.0 %collective-permute-start.12 = (bf16[160,3072]{1,0:T(8,128)(2,1)}, bf16[160,3072]{1,0:T(8,128)(2,1)}, u32[]{:S(2)}, u32[]{:S(2)}) collective-permute-start(bf16[160,3072]{1,0:T(8,128)(2,1)} %joined.8.refs_4_), channel_id=1, source_target_pairs={{0,1},{1,0},{2,3},{3,2},{4,5},{5,4},{6,7},{7,6},{8,9},{9,8},{10,11... | collective-permute-start | bytes 2949128 | tf_op jit(solution)/shard_map/ppermute | solution.py:39
  49.0 0.9 joined.9.refs_2_
  50.0 2.4 %collective-permute-start.13 = (bf16[128,3072]{1,0:T(8,128)(2,1)}, bf16[128,3072]{1,0:T(8,128)(2,1)}, u32[]{:S(2)}, u32[]{:S(2)}) collective-permute-start(bf16[128,3072]{1,0:T(8,128)(2,1)} %joined.9.refs_2_), channel_id=1, source_target_pairs={{0,1},{1,0},{2,3},{3,2},{4,5},{5,4},{6,7},{7,6},{8,9},{9,8},{10,11... | collective-permute-start | bytes 2359304 | tf_op jit(solution)/shard_map/ppermute | solution.py:39
  52.4 0.9 joined.6.refs_0_
  53.4 4.1 %collective-permute-start.7 = (bf16[128,3072]{1,0:T(8,128)(2,1)}, bf16[128,3072]{1,0:T(8,128)(2,1)}, u32[]{:S(2)}, u32[]{:S(2)}) collective-permute-start(bf16[128,3072]{1,0:T(8,128)(2,1)} %joined.6.refs_0_), channel_id=1, source_target_pairs={{0,1},{1,0},{2,3},{3,2},{4,5},{5,4},{6,7},{7,6},{8,9},{9,8},{10,11... | collective-permute-start | bytes 2359304 | tf_op jit(solution)/shard_map/ppermute | solution.py:39
  57.5 2.4 %collective-permute-start.8 = (bf16[32,3072]{1,0:T(8,128)(2,1)S(1)}, bf16[32,3072]{1,0:T(8,128)(2,1)S(1)}, u32[]{:S(2)}, u32[]{:S(2)}) collective-permute-start(bf16[32,3072]{1,0:T(8,128)(2,1)S(1)} %slice.24), channel_id=1, source_target_pairs={{0,2},{1,15},{2,4},{3,1},{4,6},{5,3},{6,8},{7,5},{8,10},{9,7},{10,... | collective-permute-start | bytes 589832 | tf_op jit(solution)/shard_map/ppermute | solution.py:43
  59.9 2.6 %collective-permute-start.9 = (bf16[32,3072]{1,0:T(8,128)(2,1)S(1)}, bf16[32,3072]{1,0:T(8,128)(2,1)S(1)}, u32[]{:S(2)}, u32[]{:S(2)}) collective-permute-start(bf16[32,3072]{1,0:T(8,128)(2,1)S(1)} %slice.25), channel_id=1, source_target_pairs={{0,2},{1,15},{2,4},{3,1},{4,6},{5,3},{6,8},{7,5},{8,10},{9,7},{10,... | collective-permute-start | bytes 589832 | tf_op jit(solution)/shard_map/ppermute | solution.py:43
  62.6 1.6 collective-permute-done.8.refs_0_
  64.2 2.5 %collective-permute-done.9.refs_1_ = bf16[32,3072]{1,0:T(8,128)(2,1)S(1)} collective-permute-done((bf16[32,3072]{1,0:T(8,128)(2,1)S(1)}, bf16[32,3072]{1,0:T(8,128)(2,1)S(1)}, u32[]{:S(2)}, u32[]{:S(2)}) %collective-permute-start.9) | collective-permute-done | bytes 196640 | tf_op jit(solution)/shard_map/ppermute | solution.py:43
  66.7 3.6 %collective-permute-start.10 = (bf16[64,3072]{1,0:T(8,128)(2,1)S(1)}, bf16[64,3072]{1,0:T(8,128)(2,1)S(1)}, u32[]{:S(2)}, u32[]{:S(2)}) collective-permute-start(bf16[64,3072]{1,0:T(8,128)(2,1)S(1)} %joined.7.refs_2_), channel_id=1, source_target_pairs={{0,1},{1,0},{2,3},{3,2},{4,5},{5,4},{6,7},{7,6},{8,9},{9,8},{10,11... | collective-permute-start | bytes 1179656 | tf_op jit(solution)/shard_map/ppermute | solution.py:39
  70.4 1.2 copy-done.1
  71.6 1.2 copy-done.3
  72.9 0.6 product.3.refs_8_
  73.5 0.5 copy-done.2
  74.1 0.3 copy-done.4
  74.4 4.0 %product.4.refs_7_ = f32[1024,512]{1,0:T(8,128)S(1)} custom-call(bf16[32,3072]{1,0:T(8,128)(2,1)S(1)} %copy-done.7, bf16[160,3072]{1,0:T(8,128)(2,1)} %collective-permute-done.12.refs_1_, bf16[128,3072]{1,0:T(8,128)(2,1)} %joined.9.refs_2_, bf16[128,3072]{1,0:T(8,128)(2,1)} %collective-permute-done.13.refs_3_, ...), custom_call_target="tpu_custom_call", output_to_operand_aliasing={{}: (8, {})} | custom-call | tf_op jit(solution)/shard_map/product/pallas_call | solution.py:205
  78.4 2.7 %product.5.values.refs_3_ = f32[1024,512]{1,0:T(8,128)S(1)} custom-call(bf16[128,3072]{1,0:T(8,128)(2,1)} %joined.6.refs_0_, bf16[128,3072]{1,0:T(8,128)(2,1)} %collective-permute-done.7.refs_1_, bf16[64,3072]{1,0:T(8,128)(2,1)S(1)} %joined.7.refs_2_, bf16[64,3072]{1,0:T(8,128)(2,1)S(1)} %collective-permute-done.10.refs_3_, ...), custom_call_target="tpu_custom_call", output_to_operand_aliasing={{}: (7, {})} | custom-call | tf_op jit(solution)/shard_map/product/pallas_call | solution.py:205
  81.2 3.1 %taken.6 = f32[6,96,512]{2,1,0:T(8,128)S(1)} custom-call(s32[3]{0:T(128)S(1)} %pad_add_fusion.me.refs_0_, s32[256]{0:T(256)S(1)} %fusion.8.first.refs_1_, s32[256]{0:T(256)S(1)} %get-tuple-element.7.turn.refs_2_, f32[1024,512]{1,0:T(8,128)S(1)} %product.5.values.refs_3_), custom_call_target="tpu_custom_call" | custom-call | tf_op jit(solution)/shard_map/taken/pallas_call | solution.py:97
  84.2 1.9 %collective-permute-start.15 = (f32[6,96,512]{2,1,0:T(8,128)S(1)}, f32[6,96,512]{2,1,0:T(8,128)S(1)}, u32[]{:S(2)}, u32[]{:S(2)}) collective-permute-start(f32[6,96,512]{2,1,0:T(8,128)S(1)} %taken.6), channel_id=1, source_target_pairs={{0,1},{1,0},{2,3},{3,2},{4,5},{5,4},{6,7},{7,6},{8,9},{9,8},{10,11... | collective-permute-start | bytes 3538952 | tf_op jit(solution)/shard_map/ppermute | solution.py:39
  86.2 1.0 taken.7
  87.2 2.4 %collective-permute-start.16 = (f32[1,96,512]{2,1,0:T(8,128)S(1)}, f32[1,96,512]{2,1,0:T(8,128)S(1)}, u32[]{:S(2)}, u32[]{:S(2)}) collective-permute-start(f32[1,96,512]{2,1,0:T(8,128)S(1)} %taken.7), channel_id=1, source_target_pairs={{0,1},{1,0},{2,3},{3,2},{4,5},{5,4},{6,7},{7,6},{8,9},{9,8},{10,11... | collective-permute-start | bytes 589832 | tf_op jit(solution)/shard_map/ppermute | solution.py:39
  89.6 1.0 collective-permute-done.16.refs_4_
  90.6 1.0 paired.7
  91.6 5.1 %collective-permute-start.17 = (f32[2,96,512]{2,1,0:T(8,128)S(1)}, f32[2,96,512]{2,1,0:T(8,128)S(1)}, u32[]{:S(2)}, u32[]{:S(2)}) collective-permute-start(f32[2,96,512]{2,1,0:T(8,128)S(1)} %paired.7), channel_id=1, source_target_pairs={{0,32},{1,225},{32,64},{33,1},{64,96},{65,33},{96,128},{97,65},{12... | collective-permute-start | bytes 1179656 | tf_op jit(solution)/shard_map/ppermute | solution.py:43
  96.7 4.7 %collective-permute-done.17.refs_5_ = f32[2,96,512]{2,1,0:T(8,128)S(1)} collective-permute-done((f32[2,96,512]{2,1,0:T(8,128)S(1)}, f32[2,96,512]{2,1,0:T(8,128)S(1)}, u32[]{:S(2)}, u32[]{:S(2)}) %collective-permute-start.17) | collective-permute-done | bytes 393248 | tf_op jit(solution)/shard_map/ppermute | solution.py:43
  101.4 1.1 paired.8
  102.5 5.0 %collective-permute-start.18 = (f32[2,96,512]{2,1,0:T(8,128)S(1)}, f32[2,96,512]{2,1,0:T(8,128)S(1)}, u32[]{:S(2)}, u32[]{:S(2)}) collective-permute-start(f32[2,96,512]{2,1,0:T(8,128)S(1)} %paired.8), channel_id=1, source_target_pairs={{0,32},{1,225},{32,64},{33,1},{64,96},{65,33},{96,128},{97,65},{12... | collective-permute-start | bytes 1179656 | tf_op jit(solution)/shard_map/ppermute | solution.py:43
  107.5 1.0 paired.11
  108.6 2.1 %collective-permute-start.21 = (f32[2,96,512]{2,1,0:T(8,128)S(1)}, f32[2,96,512]{2,1,0:T(8,128)S(1)}, u32[]{:S(2)}, u32[]{:S(2)}) collective-permute-start(f32[2,96,512]{2,1,0:T(8,128)S(1)} %paired.11), channel_id=1, source_target_pairs={{0,32},{1,225},{32,64},{33,1},{64,96},{65,33},{96,128},{97,65},{12... | collective-permute-start | bytes 1179656 | tf_op jit(solution)/shard_map/ppermute | solution.py:43
  110.6 1.6 collective-permute-done.18.refs_5_
  112.2 1.0 paired.9
  113.3 5.0 %collective-permute-start.19 = (f32[2,96,512]{2,1,0:T(8,128)S(1)}, f32[2,96,512]{2,1,0:T(8,128)S(1)}, u32[]{:S(2)}, u32[]{:S(2)}) collective-permute-start(f32[2,96,512]{2,1,0:T(8,128)S(1)} %paired.9), channel_id=1, source_target_pairs={{0,32},{1,225},{32,64},{33,1},{64,96},{65,33},{96,128},{97,65},{12... | collective-permute-start | bytes 1179656 | tf_op jit(solution)/shard_map/ppermute | solution.py:43
  118.3 1.0 paired.12
  119.3 3.2 %collective-permute-start.22 = (f32[2,96,512]{2,1,0:T(8,128)S(1)}, f32[2,96,512]{2,1,0:T(8,128)S(1)}, u32[]{:S(2)}, u32[]{:S(2)}) collective-permute-start(f32[2,96,512]{2,1,0:T(8,128)S(1)} %paired.12), channel_id=1, source_target_pairs={{0,32},{1,225},{32,64},{33,1},{64,96},{65,33},{96,128},{97,65},{12... | collective-permute-start | bytes 1179656 | tf_op jit(solution)/shard_map/ppermute | solution.py:43
  122.5 0.5 collective-permute-done.19.refs_5_
  123.0 1.0 paired.10
  124.0 7.2 %collective-permute-start.20 = (f32[2,96,512]{2,1,0:T(8,128)S(1)}, f32[2,96,512]{2,1,0:T(8,128)S(1)}, u32[]{:S(2)}, u32[]{:S(2)}) collective-permute-start(f32[2,96,512]{2,1,0:T(8,128)S(1)} %paired.10), channel_id=1, source_target_pairs={{0,288},{1,481},{32,320},{33,257},{64,352},{65,289},{96,384},{97,3... | collective-permute-start | bytes 1179656 | tf_op jit(solution)/shard_map/ppermute | solution.py:300
  131.3 1.0 paired.13
  132.3 1.9 %collective-permute-start.23 = (f32[2,96,512]{2,1,0:T(8,128)S(1)}, f32[2,96,512]{2,1,0:T(8,128)S(1)}, u32[]{:S(2)}, u32[]{:S(2)}) collective-permute-start(f32[2,96,512]{2,1,0:T(8,128)S(1)} %paired.13), channel_id=1, source_target_pairs={{0,32},{1,225},{32,64},{33,1},{64,96},{65,33},{96,128},{97,65},{12... | collective-permute-start | bytes 1179656 | tf_op jit(solution)/shard_map/ppermute | solution.py:43
  134.2 1.0 taken.5
  135.2 3.4 %collective-permute-start.14 = (f32[96,512]{1,0:T(8,128)S(1)}, f32[96,512]{1,0:T(8,128)S(1)}, u32[]{:S(2)}, u32[]{:S(2)}) collective-permute-start(f32[96,512]{1,0:T(8,128)S(1)} %bitcast.27), channel_id=1, source_target_pairs={{0,256},{256,0},{1,257},{257,1},{2,258},{258,2},{3,259},{259,3},{4... | collective-permute-start | bytes 589832 | tf_op jit(solution)/shard_map/ppermute | solution.py:292
  138.7 3.0 %collective-permute-done.23 = f32[2,96,512]{2,1,0:T(8,128)S(1)} collective-permute-done((f32[2,96,512]{2,1,0:T(8,128)S(1)}, f32[2,96,512]{2,1,0:T(8,128)S(1)}, u32[]{:S(2)}, u32[]{:S(2)}) %collective-permute-start.23) | collective-permute-done | bytes 393248 | tf_op jit(solution)/shard_map/ppermute | solution.py:43
  141.7 5.6 %collective-permute-start.24 = (f32[96,512]{1,0:T(8,128)S(1)}, f32[96,512]{1,0:T(8,128)}, u32[]{:S(2)}, u32[]{:S(2)}) collective-permute-start(f32[96,512]{1,0:T(8,128)S(1)} %fusion), channel_id=1, source_target_pairs={{0,1},{1,0},{2,3},{3,2},{4,5},{5,4},{6,7},{7,6},{8,9},{9,8},{10,11... | collective-permute-start | bytes 589832 | tf_op jit(solution)/shard_map/ppermute | solution.py:39
  147.5 1.0 taken.4
  148.5 1.1 multiply_reduce_fusion
  149.7 0.6 broadcast_in_dim.49
  150.3 4.0 %all-to-all-start = ((f32[32,1,96]{2,1,0:T(1,128)}), f32[32,1,96]{2,1,0:T(1,128)S(1)}, u32[]{:S(2)}, u32[]{:S(2)}) async-start(f32[32,1,96]{2,1,0:T(1,128)} %broadcast_in_dim.49), calls=%async_computation | async-start | bytes 32768 | tf_op jit(solution)/shard_map/all_to_all | solution.py:308
  154.5 7.6 %all-to-all-done = f32[32,1,96]{2,1,0:T(1,128)S(1)} async-done(((f32[32,1,96]{2,1,0:T(1,128)}), f32[32,1,96]{2,1,0:T(1,128)S(1)}, u32[]{:S(2)}, u32[]{:S(2)}) %all-to-all-start) | async-done | bytes 12320 | tf_op jit(solution)/shard_map/all_to_all | solution.py:308
  162.2 0.7 select_convert_fusion
  (45 shorter events, 0.8 us)
Async XLA Ops:
  2.0 10.0 %collective-permute-start = (bf16[32,3072]{1,0:T(8,128)(2,1)}, bf16[32,3072]{1,0:T(8,128)(2,1)S(1)}, u32[]{:S(2)}, u32[]{:S(2)}) collective-permute-start(bf16[32,3072]{1,0:T(8,128)(2,1)} %pick.1.refs_0_), channel_id=1, source_target_pairs={{0,1},{1,0},{2,3},{3,2},{4,5},{5,4},{6,7},{7,6},{8,9},{9,8},{10,11... | collective-permute-start | bytes 589832 | tf_op jit(solution)/shard_map/ppermute | solution.py:39
  12.1 0.9 copy-start.5
  13.0 10.0 %collective-permute-start.1 = (bf16[64,3072]{1,0:T(8,128)(2,1)S(1)}, bf16[64,3072]{1,0:T(8,128)(2,1)S(1)}, u32[]{:S(2)}, u32[]{:S(2)}) collective-permute-start(bf16[64,3072]{1,0:T(8,128)(2,1)S(1)} %joined.5.refs_0_), channel_id=1, source_target_pairs={{0,2},{1,15},{2,4},{3,1},{4,6},{5,3},{6,8},{7,5},{8,10},{9,7},{10,... | collective-permute-start | bytes 1179656 | tf_op jit(solution)/shard_map/ppermute | solution.py:43
  18.3 13.3 %collective-permute-start.4 = (bf16[64,3072]{1,0:T(8,128)(2,1)S(1)}, bf16[64,3072]{1,0:T(8,128)(2,1)S(1)}, u32[]{:S(2)}, u32[]{:S(2)}) collective-permute-start(bf16[64,3072]{1,0:T(8,128)(2,1)S(1)} %joined.5.refs_0_), channel_id=1, source_target_pairs={{0,18},{1,31},{2,20},{3,17},{4,22},{5,19},{6,24},{7,21},{8,26},{9,... | collective-permute-start | bytes 1179656 | tf_op jit(solution)/shard_map/ppermute | solution.py:230
  23.0 15.4 %collective-permute-start.2 = (bf16[64,3072]{1,0:T(8,128)(2,1)S(1)}, bf16[64,3072]{1,0:T(8,128)(2,1)S(1)}, u32[]{:S(2)}, u32[]{:S(2)}) collective-permute-start(bf16[64,3072]{1,0:T(8,128)(2,1)S(1)} %collective-permute-done.1.refs_0_), channel_id=1, source_target_pairs={{0,2},{1,15},{2,4},{3,1},{4,6},{5,3},{6,8},{7,5},{8,10},{9,7},{10,... | collective-permute-start | bytes 1179656 | tf_op jit(solution)/shard_map/ppermute | solution.py:43
  31.6 9.3 %collective-permute-start.5 = (bf16[64,3072]{1,0:T(8,128)(2,1)S(1)}, bf16[64,3072]{1,0:T(8,128)(2,1)S(1)}, u32[]{:S(2)}, u32[]{:S(2)}) collective-permute-start(bf16[64,3072]{1,0:T(8,128)(2,1)S(1)} %collective-permute-done.4.refs_1_), channel_id=1, source_target_pairs={{0,2},{1,15},{2,4},{3,1},{4,6},{5,3},{6,8},{7,5},{8,10},{9,7},{10,... | collective-permute-start | bytes 1179656 | tf_op jit(solution)/shard_map/ppermute | solution.py:43
  36.2 9.7 %collective-permute-start.11 = (bf16[32,3072]{1,0:T(8,128)(2,1)S(1)}, bf16[32,3072]{1,0:T(8,128)(2,1)S(1)}, u32[]{:S(2)}, u32[]{:S(2)}) collective-permute-start(bf16[32,3072]{1,0:T(8,128)(2,1)S(1)} %copy-done.5), channel_id=1, source_target_pairs={{0,16},{16,0},{1,17},{17,1},{2,18},{18,2},{3,19},{19,3},{4,20},{20... | collective-permute-start | bytes 589832 | tf_op jit(solution)/shard_map/ppermute | solution.py:231
  38.4 14.0 %collective-permute-start.3 = (bf16[64,3072]{1,0:T(8,128)(2,1)S(1)}, bf16[64,3072]{1,0:T(8,128)(2,1)S(1)}, u32[]{:S(2)}, u32[]{:S(2)}) collective-permute-start(bf16[64,3072]{1,0:T(8,128)(2,1)S(1)} %collective-permute-done.2.refs_0_), channel_id=1, source_target_pairs={{0,2},{1,15},{2,4},{3,1},{4,6},{5,3},{6,8},{7,5},{8,10},{9,7},{10,... | collective-permute-start | bytes 1179656 | tf_op jit(solution)/shard_map/ppermute | solution.py:43
  40.9 11.5 %collective-permute-start.6 = (bf16[64,3072]{1,0:T(8,128)(2,1)S(1)}, bf16[64,3072]{1,0:T(8,128)(2,1)S(1)}, u32[]{:S(2)}, u32[]{:S(2)}) collective-permute-start(bf16[64,3072]{1,0:T(8,128)(2,1)S(1)} %collective-permute-done.5.refs_1_), channel_id=1, source_target_pairs={{0,2},{1,15},{2,4},{3,1},{4,6},{5,3},{6,8},{7,5},{8,10},{9,7},{10,... | collective-permute-start | bytes 1179656 | tf_op jit(solution)/shard_map/ppermute | solution.py:43
  45.9 7.4 %copy-start.6 = (bf16[32,3072]{1,0:T(8,128)(2,1)}, bf16[32,3072]{1,0:T(8,128)(2,1)S(1)}, u32[]{:S(2)}) copy-start(bf16[32,3072]{1,0:T(8,128)(2,1)S(1)} %collective-permute-done.11.refs_2_.refs_0_) | copy-start | bytes 589828
  47.0 23.3 %copy-start.9 = (s32[256]{0:T(256)S(1)}, s32[256]{0:T(256)}, u32[]{:S(2)}) copy-start(s32[256]{0:T(256)} %param.17) | copy-start | bytes 3076
  47.0 23.4 %copy-start = (bf16[1024,512]{1,0:T(8,128)(2,1)S(1)}, bf16[1024,512]{1,0:T(8,128)(2,1)}, u32[]{:S(2)}) copy-start(bf16[1024,512]{1,0:T(8,128)(2,1)} %refs_4_.1) | copy-start | bytes 3145732
  47.0 26.5 %collective-permute-start.12 = (bf16[160,3072]{1,0:T(8,128)(2,1)}, bf16[160,3072]{1,0:T(8,128)(2,1)}, u32[]{:S(2)}, u32[]{:S(2)}) collective-permute-start(bf16[160,3072]{1,0:T(8,128)(2,1)} %joined.8.refs_4_), channel_id=1, source_target_pairs={{0,1},{1,0},{2,3},{3,2},{4,5},{5,4},{6,7},{7,6},{8,9},{9,8},{10,11... | collective-permute-start | bytes 2949128 | tf_op jit(solution)/shard_map/ppermute | solution.py:39
  50.0 23.5 %collective-permute-start.13 = (bf16[128,3072]{1,0:T(8,128)(2,1)}, bf16[128,3072]{1,0:T(8,128)(2,1)}, u32[]{:S(2)}, u32[]{:S(2)}) collective-permute-start(bf16[128,3072]{1,0:T(8,128)(2,1)} %joined.9.refs_2_), channel_id=1, source_target_pairs={{0,1},{1,0},{2,3},{3,2},{4,5},{5,4},{6,7},{7,6},{8,9},{9,8},{10,11... | collective-permute-start | bytes 2359304 | tf_op jit(solution)/shard_map/ppermute | solution.py:39
  53.4 25.0 %collective-permute-start.7 = (bf16[128,3072]{1,0:T(8,128)(2,1)}, bf16[128,3072]{1,0:T(8,128)(2,1)}, u32[]{:S(2)}, u32[]{:S(2)}) collective-permute-start(bf16[128,3072]{1,0:T(8,128)(2,1)} %joined.6.refs_0_), channel_id=1, source_target_pairs={{0,1},{1,0},{2,3},{3,2},{4,5},{5,4},{6,7},{7,6},{8,9},{9,8},{10,11... | collective-permute-start | bytes 2359304 | tf_op jit(solution)/shard_map/ppermute | solution.py:39
  57.5 6.7 %collective-permute-start.8 = (bf16[32,3072]{1,0:T(8,128)(2,1)S(1)}, bf16[32,3072]{1,0:T(8,128)(2,1)S(1)}, u32[]{:S(2)}, u32[]{:S(2)}) collective-permute-start(bf16[32,3072]{1,0:T(8,128)(2,1)S(1)} %slice.24), channel_id=1, source_target_pairs={{0,2},{1,15},{2,4},{3,1},{4,6},{5,3},{6,8},{7,5},{8,10},{9,7},{10,... | collective-permute-start | bytes 589832 | tf_op jit(solution)/shard_map/ppermute | solution.py:43
  59.9 6.7 %collective-permute-start.9 = (bf16[32,3072]{1,0:T(8,128)(2,1)S(1)}, bf16[32,3072]{1,0:T(8,128)(2,1)S(1)}, u32[]{:S(2)}, u32[]{:S(2)}) collective-permute-start(bf16[32,3072]{1,0:T(8,128)(2,1)S(1)} %slice.25), channel_id=1, source_target_pairs={{0,2},{1,15},{2,4},{3,1},{4,6},{5,3},{6,8},{7,5},{8,10},{9,7},{10,... | collective-permute-start | bytes 589832 | tf_op jit(solution)/shard_map/ppermute | solution.py:43
  66.7 11.7 %collective-permute-start.10 = (bf16[64,3072]{1,0:T(8,128)(2,1)S(1)}, bf16[64,3072]{1,0:T(8,128)(2,1)S(1)}, u32[]{:S(2)}, u32[]{:S(2)}) collective-permute-start(bf16[64,3072]{1,0:T(8,128)(2,1)S(1)} %joined.7.refs_2_), channel_id=1, source_target_pairs={{0,1},{1,0},{2,3},{3,2},{4,5},{5,4},{6,7},{7,6},{8,9},{9,8},{10,11... | collective-permute-start | bytes 1179656 | tf_op jit(solution)/shard_map/ppermute | solution.py:39
  70.4 1.2 copy-start.1
  71.6 1.2 copy-start.3
  72.9 1.2 copy-start.2
  72.9 1.5 copy-start.4
  72.9 1.6 copy-start.7
  84.2 17.2 %collective-permute-start.15 = (f32[6,96,512]{2,1,0:T(8,128)S(1)}, f32[6,96,512]{2,1,0:T(8,128)S(1)}, u32[]{:S(2)}, u32[]{:S(2)}) collective-permute-start(f32[6,96,512]{2,1,0:T(8,128)S(1)} %taken.6), channel_id=1, source_target_pairs={{0,1},{1,0},{2,3},{3,2},{4,5},{5,4},{6,7},{7,6},{8,9},{9,8},{10,11... | collective-permute-start | bytes 3538952 | tf_op jit(solution)/shard_map/ppermute | solution.py:39
  87.2 3.5 %collective-permute-start.16 = (f32[1,96,512]{2,1,0:T(8,128)S(1)}, f32[1,96,512]{2,1,0:T(8,128)S(1)}, u32[]{:S(2)}, u32[]{:S(2)}) collective-permute-start(f32[1,96,512]{2,1,0:T(8,128)S(1)} %taken.7), channel_id=1, source_target_pairs={{0,1},{1,0},{2,3},{3,2},{4,5},{5,4},{6,7},{7,6},{8,9},{9,8},{10,11... | collective-permute-start | bytes 589832 | tf_op jit(solution)/shard_map/ppermute | solution.py:39
  91.6 9.8 %collective-permute-start.17 = (f32[2,96,512]{2,1,0:T(8,128)S(1)}, f32[2,96,512]{2,1,0:T(8,128)S(1)}, u32[]{:S(2)}, u32[]{:S(2)}) collective-permute-start(f32[2,96,512]{2,1,0:T(8,128)S(1)} %paired.7), channel_id=1, source_target_pairs={{0,32},{1,225},{32,64},{33,1},{64,96},{65,33},{96,128},{97,65},{12... | collective-permute-start | bytes 1179656 | tf_op jit(solution)/shard_map/ppermute | solution.py:43
  102.5 9.7 %collective-permute-start.18 = (f32[2,96,512]{2,1,0:T(8,128)S(1)}, f32[2,96,512]{2,1,0:T(8,128)S(1)}, u32[]{:S(2)}, u32[]{:S(2)}) collective-permute-start(f32[2,96,512]{2,1,0:T(8,128)S(1)} %paired.8), channel_id=1, source_target_pairs={{0,32},{1,225},{32,64},{33,1},{64,96},{65,33},{96,128},{97,65},{12... | collective-permute-start | bytes 1179656 | tf_op jit(solution)/shard_map/ppermute | solution.py:43
  108.6 9.7 %collective-permute-start.21 = (f32[2,96,512]{2,1,0:T(8,128)S(1)}, f32[2,96,512]{2,1,0:T(8,128)S(1)}, u32[]{:S(2)}, u32[]{:S(2)}) collective-permute-start(f32[2,96,512]{2,1,0:T(8,128)S(1)} %paired.11), channel_id=1, source_target_pairs={{0,32},{1,225},{32,64},{33,1},{64,96},{65,33},{96,128},{97,65},{12... | collective-permute-start | bytes 1179656 | tf_op jit(solution)/shard_map/ppermute | solution.py:43
  113.3 9.7 %collective-permute-start.19 = (f32[2,96,512]{2,1,0:T(8,128)S(1)}, f32[2,96,512]{2,1,0:T(8,128)S(1)}, u32[]{:S(2)}, u32[]{:S(2)}) collective-permute-start(f32[2,96,512]{2,1,0:T(8,128)S(1)} %paired.9), channel_id=1, source_target_pairs={{0,32},{1,225},{32,64},{33,1},{64,96},{65,33},{96,128},{97,65},{12... | collective-permute-start | bytes 1179656 | tf_op jit(solution)/shard_map/ppermute | solution.py:43
  119.3 11.9 %collective-permute-start.22 = (f32[2,96,512]{2,1,0:T(8,128)S(1)}, f32[2,96,512]{2,1,0:T(8,128)S(1)}, u32[]{:S(2)}, u32[]{:S(2)}) collective-permute-start(f32[2,96,512]{2,1,0:T(8,128)S(1)} %paired.12), channel_id=1, source_target_pairs={{0,32},{1,225},{32,64},{33,1},{64,96},{65,33},{96,128},{97,65},{12... | collective-permute-start | bytes 1179656 | tf_op jit(solution)/shard_map/ppermute | solution.py:43
  124.0 14.6 %collective-permute-start.20 = (f32[2,96,512]{2,1,0:T(8,128)S(1)}, f32[2,96,512]{2,1,0:T(8,128)S(1)}, u32[]{:S(2)}, u32[]{:S(2)}) collective-permute-start(f32[2,96,512]{2,1,0:T(8,128)S(1)} %paired.10), channel_id=1, source_target_pairs={{0,288},{1,481},{32,320},{33,257},{64,352},{65,289},{96,384},{97,3... | collective-permute-start | bytes 1179656 | tf_op jit(solution)/shard_map/ppermute | solution.py:300
  132.3 15.1 %copy-start.8 = (s32[256]{0:T(256)S(1)}, s32[256]{0:T(256)}, u32[]{:S(2)}) copy-start(s32[256]{0:T(256)} %accepted.1) | copy-start | bytes 3076
  132.3 9.3 %collective-permute-start.23 = (f32[2,96,512]{2,1,0:T(8,128)S(1)}, f32[2,96,512]{2,1,0:T(8,128)S(1)}, u32[]{:S(2)}, u32[]{:S(2)}) collective-permute-start(f32[2,96,512]{2,1,0:T(8,128)S(1)} %paired.13), channel_id=1, source_target_pairs={{0,32},{1,225},{32,64},{33,1},{64,96},{65,33},{96,128},{97,65},{12... | collective-permute-start | bytes 1179656 | tf_op jit(solution)/shard_map/ppermute | solution.py:43
  135.2 26.9 %copy-start.10 = (f32[512]{0:T(512)S(1)}, f32[512]{0:T(512)}, u32[]{:S(2)}) copy-start(f32[512]{0:T(512)} %param.15) | copy-start | bytes 6148
  135.2 13.3 %collective-permute-start.14 = (f32[96,512]{1,0:T(8,128)S(1)}, f32[96,512]{1,0:T(8,128)S(1)}, u32[]{:S(2)}, u32[]{:S(2)}) collective-permute-start(f32[96,512]{1,0:T(8,128)S(1)} %bitcast.27), channel_id=1, source_target_pairs={{0,256},{256,0},{1,257},{257,1},{2,258},{258,2},{3,259},{259,3},{4... | collective-permute-start | bytes 589832 | tf_op jit(solution)/shard_map/ppermute | solution.py:292
  141.7 6.9 %collective-permute-start.24 = (f32[96,512]{1,0:T(8,128)S(1)}, f32[96,512]{1,0:T(8,128)}, u32[]{:S(2)}, u32[]{:S(2)}) collective-permute-start(f32[96,512]{1,0:T(8,128)S(1)} %fusion), channel_id=1, source_target_pairs={{0,1},{1,0},{2,3},{3,2},{4,5},{5,4},{6,7},{7,6},{8,9},{9,8},{10,11... | collective-permute-start | bytes 589832 | tf_op jit(solution)/shard_map/ppermute | solution.py:39
  150.3 11.8 %all-to-all-start = ((f32[32,1,96]{2,1,0:T(1,128)}), f32[32,1,96]{2,1,0:T(1,128)S(1)}, u32[]{:S(2)}, u32[]{:S(2)}) async-start(f32[32,1,96]{2,1,0:T(1,128)} %broadcast_in_dim.49), calls=%async_computation | async-start | bytes 32768 | tf_op jit(solution)/shard_map/all_to_all | solution.py:308
where the time goes:
time: 164 us; the launch traced here: 163 us
  starting transfers between devices  99.9 us (61%)
  waiting for transfers between devices  29.5 us (18%)
  Pallas kernels  25.6 us (16%)
  local copies, waits for them, and re-layouts  5.11 us (3%)
  other arithmetic  2.31 us (1%)
    ppermute x13, starting transfers between devices, onward(): return lax.ppermute(x, (axis, 'c'), both_ways(lax.axis_size(axis)))  49.1 us
    ppermute x8, starting transfers between devices, other_core(): return lax.ppermute(x, 'c', SWAP)  30.8 us
    ppermute x13, waiting for transfers between devices, onward(): return lax.ppermute(x, (axis, 'c'), both_ways(lax.axis_size(axis)))  15.9 us
    all_to_all x1, waiting for transfers between devices, step_on_device(): lax.all_to_all(jnp.broadcast_to(squares[None], (4 * nz, size)), GRP, 0, 0...  7.61 us
    pallas_call x3, Pallas kernels, product(): pl.pallas_call(kernel, out_shape=jax.ShapeDtypeStruct((rows, columns), jn...  7.34 us
    ppermute x1, starting transfers between devices, step_on_device(): came[v] = lax.ppermute(total, (*TP, 'c'), diagonal(ny))  7.21 us
    pallas_call x7, Pallas kernels, paired(): pl.pallas_call(kernel, out_shape=jax.ShapeDtypeStruct((2, *theirs.shape[1...  7.21 us
    pallas_call x4, Pallas kernels, taken(): pl.pallas_call(kernel, out_shape=jax.ShapeDtypeStruct((len(blocks), first...  6.02 us
  transfers between devices with their start and end apart: 26, of which 12 were waited for; matrix products, arithmetic and copies ran while one was open for 0% of the time, Pallas kernels for 10%

commit v1 on v0

--- a/solution.py
+++ b/solution.py
@@ -45,6 +45,7 @@
 
 VMEM = pl.BlockSpec(memory_space=pltpu.VMEM)
 SMEM = pl.BlockSpec(memory_space=pltpu.SMEM)
+HBM = pl.BlockSpec(memory_space=pltpu.HBM)
 SMALL = pltpu.CompilerParams(vmem_limit_bytes=8 << 20)
 
 
@@ -64,6 +65,20 @@
         compiler_params=SMALL,
         name="joined",
     )(*parts)
+
+
+def upper(x, rows):
+    def kernel(x, out):
+        out[...] = x[:rows]
+
+    return pl.pallas_call(
+        kernel,
+        out_shape=jax.ShapeDtypeStruct((rows, x.shape[1]), x.dtype),
+        in_specs=[VMEM],
+        out_specs=VMEM,
+        compiler_params=SMALL,
+        name="upper",
+    )(x)
 
 
 def each_row(me, first, turn, values, block, do):
@@ -136,7 +151,7 @@
     )(*table, theirs, *more)
 
 
-def pick_kernel(group, accepted, low, mid, high, out, used_by, held, sems):
+def pick_kernel(me, accepted, low, mid, high, out, used_by, held, sems):
     feats = (low, mid, high)
     copies = [pltpu.make_async_copy(accepted, used_by, sems.at[3])]
     copies += [pltpu.make_async_copy(f, held.at[i], sems.at[i]) for i, f in enumerate(feats)]
@@ -149,7 +164,7 @@
     used = jnp.zeros_like(slot)
     copies[0].wait()
     for i in range(ROWS_G // 2):
-        used = jnp.where(pair == i, used_by[group[0] * ROWS_G + 2 * i] + 1, used)
+        used = jnp.where(pair == i, used_by[me[3] * ROWS_G + 2 * i] + 1, used)
     source = pair * (2 * POS) + jnp.where(at < used, at, 2 * POS + 1 - at)
     pick = jnp.where(source == token, 1.0, 0.0).astype(jnp.bfloat16)
     for i in range(3):
@@ -159,57 +174,74 @@
         ).astype(jnp.bfloat16)
 
 
-def selected(feats, group, accepted):
+def selected(feats, me, accepted):
     slots, width = ROWS_G // 2 * SLOTS, 3 * feats[0].shape[1]
     return pl.pallas_call(
         pick_kernel,
         out_shape=jax.ShapeDtypeStruct((slots, width), jnp.bfloat16),
-        in_specs=[SMEM] + [pl.BlockSpec(memory_space=pl.ANY)] * 4,
+        in_specs=[SMEM] + [HBM] * 4,
         out_specs=VMEM,
         scratch_shapes=[
             pltpu.SMEM(accepted.shape, jnp.int32),
             pltpu.VMEM((3, *feats[0].shape), jnp.bfloat16),
             pltpu.SemaphoreType.DMA((4,)),
         ],
-        compiler_params=pltpu.CompilerParams(vmem_limit_bytes=60 << 20),
+        compiler_params=SMALL,
         name="pick",
-    )(group[None], accepted, *feats)
+    )(me, *(pltpu.with_memory_space_constraint(x, pltpu.HBM) for x in (accepted, *feats)))
 
 
 def product(parts, weights, rows, at, before=None):
-    k, columns = weights[0].shape
+    columns = weights[0].shape[1]
     count = sum(n for _, _, n in parts)
-
     arrays = []
     for p, _, _ in parts:
         if not any(p is q for q in arrays):
             arrays.append(p)
     which = [next(i for i, q in enumerate(arrays) if q is p) for p, _, _ in parts]
+    depth = arrays[0].shape[1]
 
     def kernel(*refs):
         n = len(arrays)
-        ws, out, held = refs[n : n + 3], refs[-2], refs[-1]
+        if before is None:
+            out, near, held, sems = refs[-4:]
+            k = depth // 3
+            copies = [
+                pltpu.make_async_copy(refs[n + i], near.at[pl.ds(i * k, k)], sems.at[i])
+                for i in range(3)
+            ]
+            for copy in copies:
+                copy.start()
+        else:
+            near, (out, _, held) = refs[n], refs[-3:]
         to = 0
         for i, (_, start, number) in zip(which, parts, strict=True):
             held[to : to + number] = refs[i][start : start + number]
             to += number
-        total = jnp.dot(held[:, :k], ws[0][...], preferred_element_type=jnp.float32)
-        for i in (1, 2):
-            total += jnp.dot(
-                held[:, i * k : (i + 1) * k], ws[i][...], preferred_element_type=jnp.float32
-            )
-        out[at : at + count] = total
-
+        if before is None:
+            for copy in copies:
+                copy.wait()
+        out[at : at + count] = jnp.dot(
+            held[...], near[...], preferred_element_type=jnp.float32
+        )
+
+    if before is None:
+        weights = [pltpu.with_memory_space_constraint(w, pltpu.HBM) for w in weights]
     operands = arrays + list(weights)
-    aliases = {} if before is None else {len(operands): 0}
-    return pl.pallas_call(
-        kernel,
-        out_shape=jax.ShapeDtypeStruct((rows, columns), jnp.float32),
-        in_specs=[VMEM] * (len(operands) + len(aliases)),
-        out_specs=VMEM,
-        scratch_shapes=[pltpu.VMEM((count, 3 * k), jnp.bfloat16)],
+    aliases = {} if before is None else {len(operands): 0, len(arrays): 1}
+    shapes = (
+        jax.ShapeDtypeStruct((rows, columns), jnp.float32),
+        jax.ShapeDtypeStruct((depth, columns), jnp.bfloat16),
+    )
+    return pl.pallas_call(
+        kernel,
+        out_shape=shapes,
+        in_specs=[VMEM] * len(arrays) + ([HBM] * 3 if before is None else [VMEM] * 2),
+        out_specs=(VMEM,) * len(shapes),
+        scratch_shapes=[pltpu.VMEM((count, depth), jnp.bfloat16)]
+        + ([pltpu.SemaphoreType.DMA((3,))] if before is None else []),
         input_output_aliases=aliases,
-        compiler_params=pltpu.CompilerParams(vmem_limit_bytes=12 << 20),
+        compiler_params=pltpu.CompilerParams(vmem_limit_bytes=6 << 20),
         name="product",
     )(*operands, *([] if before is None else [before]))
 
@@ -222,7 +254,8 @@
     ny, nz = lax.axis_size("y"), lax.axis_size("z")
     way = 1 - 2 * c
     group = (xl * nz + z) * 2 + c
-    mine = selected((low_feats, mid_feats, high_feats), group, accepted)
+    me = lax.optimization_barrier(jnp.stack([xh, y, c, group, xl, z, way]))
+    mine = selected((low_feats, mid_feats, high_feats), me, accepted)
     block = mine.shape[0]
 
     chip = joined(mine, other_core(mine))
@@ -232,15 +265,17 @@
     for _ in range(2):
         straight.append(onward(straight[-1], "z"))
         crossed.append(onward(crossed[-1], "z"))
-    straight.append(onward(straight[-1][:block], "z"))
-    crossed.append(onward(crossed[-1][:block], "z"))
+    half = upper(straight[-1], block)
+    straight.append(onward(half, "z"))
+    half = upper(crossed[-1], block)
+    crossed.append(onward(half, "z"))
     here, there = [], []
     for s in range(4):
         here.append(joined(straight[s], crossed[s], *((beside,) if s == 1 else ())))
         there.append(other_core(here[s]))
     cut = 4 * block
     total = 32 * block
-    partial_value = product([(chip, 0, 2 * block)], weights, total, 0)
+    partial_value, near = product([(chip, 0, 2 * block)], weights, total, 0)
     parts = [
         (beside, 0, block),
         (there[1], cut, block),
@@ -249,21 +284,18 @@
         (here[1], 0, cut),
         (there[1], 0, cut),
     ]
-    partial_value = product(parts, weights, total, 2 * block, partial_value)
-    parts = [
-        (here[2], 0, cut),
-        (there[2], 0, cut),
-        (here[3], 0, 2 * block),
-        (there[3], 0, 2 * block),
-    ]
-    partial_value = product(parts, weights, total, 20 * block, partial_value)
+    partial_value, near = product(parts, (near,), total, 2 * block, partial_value)
+    parts = [(here[2], 0, cut), (there[2], 0, cut)]
+    partial_value, near = product(parts, (near,), total, 20 * block, partial_value)
+    parts = [(here[3], 0, 2 * block), (there[3], 0, 2 * block)]
+    partial_value, near = product(parts, (near,), total, 28 * block, partial_value)
 
     per_slab = assignment.shape[0] // (2 * ny)
     target = assignment
     of_group = target // ROWS_G
     there_c, there_z, there_x = of_group % 2, (of_group // 2) % nz, of_group // (2 * nz)
-    dx, dc, dz = there_x ^ xl, there_c ^ c, (there_z - z) % nz
-    step = (-way * dz) % nz
+    dx, dc, dz = there_x ^ me[4], there_c ^ me[2], (there_z - me[5]) % nz
+    step = (nz - me[6] * dz) % nz
     near = jnp.minimum(step, nz - step)
     from_here = step < nz // 2
     place = jnp.where(
@@ -281,7 +313,7 @@
     turn = jnp.where(even, 1, -1)
     size = per_slab * POS
 
-    table = (jnp.stack([xh, y, c]), first, turn, partial_value)
+    table = (me, first, turn, partial_value)
     far = taken(table, (1,))
     behind = taken(table, tuple(range(2, 8)))
     beyond = taken(table, (8,))[0]

time: 164 us -> 160 us (0.976)
  Pallas kernels: 25.6 us -> 21.5 us
  local copies, waits for them, and re-layouts: 5.11 us -> 1.58 us
  other arithmetic: 2.31 us -> 4.84 us
    unnamed x22 -> x6, local copies, waits for them, and re-layouts: 4.28 us -> 0.02 us
    pallas_call x5, Pallas kernels: 2.98 us -> 0.22 us  [joined(): pl.pallas_call(kernel, out_shape=jax.ShapeDtypeStruct(shape, parts[0].dty...]
    add x1, other arithmetic: 0.05 us -> 2.67 us  [step_on_device(): place * block + in_group // 2 * SLOTS + jnp.where(even, 0, SLOTS - 1)]
    pallas_call x3 -> x6, Pallas kernels: 7.34 us -> 6.14 us  [the longest x4 6.11 us: product(): pl.pallas_call(kernel, out_shape=shapes, in_specs=[VMEM] * len(arrays) +...]
  transfers between devices with their start and end apart: 26 -> 26, of which waited for: 12 -> 13; matrix products, arithmetic and copies ran while one was open for 0% -> 2% of each run, Pallas kernels for 10% -> 9%
where the time goes in v1:
time: 160 us
  starting transfers between devices  101 us (63%)
  waiting for transfers between devices  30.3 us (19%)
  Pallas kernels  21.5 us (13%)
  other arithmetic  4.84 us (3%)
    ppermute x13, starting transfers between devices, onward(): return lax.ppermute(x, (axis, 'c'), both_ways(lax.axis_size(axis)))  49.1 us
    ppermute x8, starting transfers between devices, other_core(): return lax.ppermute(x, 'c', SWAP)  31.7 us
    ppermute x13, waiting for transfers between devices, onward(): return lax.ppermute(x, (axis, 'c'), both_ways(lax.axis_size(axis)))  17 us
    all_to_all x1, waiting for transfers between devices, step_on_device(): lax.all_to_all(jnp.broadcast_to(squares[None], (4 * nz, size)), GRP, 0, 0...  7.61 us
    pallas_call x7, Pallas kernels, paired(): pl.pallas_call(kernel, out_shape=jax.ShapeDtypeStruct((2, *theirs.shape[1...  7.22 us
    ppermute x1, starting transfers between devices, step_on_device(): came[v] = lax.ppermute(total, (*TP, 'c'), diagonal(ny))  7.2 us
    pallas_call x4, Pallas kernels, product(): pl.pallas_call(kernel, out_shape=shapes, in_specs=[VMEM] * len(arrays) +...  6.11 us
    pallas_call x4, Pallas kernels, taken(): pl.pallas_call(kernel, out_shape=jax.ShapeDtypeStruct((len(blocks), first...  6.02 us
  transfers between devices with their start and end apart: 26, of which 13 were waited for; matrix products, arithmetic and copies ran while one was open for 2% of the time, Pallas kernels for 9%

profile of v1, /device:TPU:1, one launch (start us, length us, event | category | flops | bytes accessed | tf_op | source)
XLA Modules:
  0.0 159.5 jit_solution(12364772237730699398)
XLA Ops:
  0.0 0.1 stack.31.me.refs_0_
  0.1 1.9 %pick.1.refs_0_ = bf16[32,3072]{1,0:T(8,128)(2,1)S(1)} custom-call(s32[7]{0:T(128)S(1)} %stack.31.me.refs_0_, s32[256]{0:T(256)} %accepted.1, bf16[48,1024]{1,0:T(8,128)(2,1)} %low.1, bf16[48,1024]{1,0:T(8,128)(2,1)} %mid.1, bf16[48,1024]{1,0:T(8,128)(2,1)} %high.1), custom_call_target="tpu_custom_call" | custom-call | tf_op jit(solution)/shard_map/pick/pallas_call | solution.py:179
  2.0 8.7 %collective-permute-start = (bf16[32,3072]{1,0:T(8,128)(2,1)S(1)}, bf16[32,3072]{1,0:T(8,128)(2,1)S(1)}, u32[]{:S(2)}, u32[]{:S(2)}) collective-permute-start(bf16[32,3072]{1,0:T(8,128)(2,1)S(1)} %pick.1.refs_0_), channel_id=1, source_target_pairs={{0,1},{1,0},{2,3},{3,2},{4,5},{5,4},{6,7},{7,6},{8,9},{9,8},{10,11... | collective-permute-start | bytes 589832 | tf_op jit(solution)/shard_map/ppermute | solution.py:39
  10.7 1.0 collective-permute-done.refs_1_
  11.8 5.3 %collective-permute-start.1 = (bf16[64,3072]{1,0:T(8,128)(2,1)S(1)}, bf16[64,3072]{1,0:T(8,128)(2,1)S(1)}, u32[]{:S(2)}, u32[]{:S(2)}) collective-permute-start(bf16[64,3072]{1,0:T(8,128)(2,1)S(1)} %joined.5.refs_0_), channel_id=1, source_target_pairs={{0,2},{1,15},{2,4},{3,1},{4,6},{5,3},{6,8},{7,5},{8,10},{9,7},{10,... | collective-permute-start | bytes 1179656 | tf_op jit(solution)/shard_map/ppermute | solution.py:43
  17.2 3.1 %collective-permute-start.5 = (bf16[64,3072]{1,0:T(8,128)(2,1)S(1)}, bf16[64,3072]{1,0:T(8,128)(2,1)S(1)}, u32[]{:S(2)}, u32[]{:S(2)}) collective-permute-start(bf16[64,3072]{1,0:T(8,128)(2,1)S(1)} %joined.5.refs_0_), channel_id=1, source_target_pairs={{0,18},{1,31},{2,20},{3,17},{4,22},{5,19},{6,24},{7,21},{8,26},{9,... | collective-permute-start | bytes 1179656 | tf_op jit(solution)/shard_map/ppermute | solution.py:263
  20.3 1.6 collective-permute-done.1.refs_0_
  21.9 5.0 %collective-permute-start.2 = (bf16[64,3072]{1,0:T(8,128)(2,1)S(1)}, bf16[64,3072]{1,0:T(8,128)(2,1)S(1)}, u32[]{:S(2)}, u32[]{:S(2)}) collective-permute-start(bf16[64,3072]{1,0:T(8,128)(2,1)S(1)} %collective-permute-done.1.refs_0_), channel_id=1, source_target_pairs={{0,2},{1,15},{2,4},{3,1},{4,6},{5,3},{6,8},{7,5},{8,10},{9,7},{10,... | collective-permute-start | bytes 1179656 | tf_op jit(solution)/shard_map/ppermute | solution.py:43
  26.9 3.6 %collective-permute-done.5.refs_1_ = bf16[64,3072]{1,0:T(8,128)(2,1)S(1)} collective-permute-done((bf16[64,3072]{1,0:T(8,128)(2,1)S(1)}, bf16[64,3072]{1,0:T(8,128)(2,1)S(1)}, u32[]{:S(2)}, u32[]{:S(2)}) %collective-permute-start.5) | collective-permute-done | bytes 393248 | tf_op jit(solution)/shard_map/ppermute | solution.py:263
  30.4 4.6 %collective-permute-start.6 = (bf16[64,3072]{1,0:T(8,128)(2,1)S(1)}, bf16[64,3072]{1,0:T(8,128)(2,1)S(1)}, u32[]{:S(2)}, u32[]{:S(2)}) collective-permute-start(bf16[64,3072]{1,0:T(8,128)(2,1)S(1)} %collective-permute-done.5.refs_1_), channel_id=1, source_target_pairs={{0,2},{1,15},{2,4},{3,1},{4,6},{5,3},{6,8},{7,5},{8,10},{9,7},{10,... | collective-permute-start | bytes 1179656 | tf_op jit(solution)/shard_map/ppermute | solution.py:43
  35.0 2.2 %collective-permute-start.11 = (bf16[32,3072]{1,0:T(8,128)(2,1)S(1)}, bf16[32,3072]{1,0:T(8,128)(2,1)S(1)}, u32[]{:S(2)}, u32[]{:S(2)}) collective-permute-start(bf16[32,3072]{1,0:T(8,128)(2,1)S(1)} %pick.1.refs_0_), channel_id=1, source_target_pairs={{0,16},{16,0},{1,17},{17,1},{2,18},{18,2},{3,19},{19,3},{4,20},{20... | collective-permute-start | bytes 589832 | tf_op jit(solution)/shard_map/ppermute | solution.py:264
  37.2 1.9 %collective-permute-start.3 = (bf16[64,3072]{1,0:T(8,128)(2,1)S(1)}, bf16[64,3072]{1,0:T(8,128)(2,1)S(1)}, u32[]{:S(2)}, u32[]{:S(2)}) collective-permute-start(bf16[64,3072]{1,0:T(8,128)(2,1)S(1)} %collective-permute-done.2.refs_0_), channel_id=1, source_target_pairs={{0,2},{1,15},{2,4},{3,1},{4,6},{5,3},{6,8},{7,5},{8,10},{9,7},{10,... | collective-permute-start | bytes 1179656 | tf_op jit(solution)/shard_map/ppermute | solution.py:43
  39.1 0.6 collective-permute-done.6.refs_1_
  39.7 5.0 %collective-permute-start.7 = (bf16[64,3072]{1,0:T(8,128)(2,1)S(1)}, bf16[64,3072]{1,0:T(8,128)(2,1)S(1)}, u32[]{:S(2)}, u32[]{:S(2)}) collective-permute-start(bf16[64,3072]{1,0:T(8,128)(2,1)S(1)} %collective-permute-done.6.refs_1_), channel_id=1, source_target_pairs={{0,2},{1,15},{2,4},{3,1},{4,6},{5,3},{6,8},{7,5},{8,10},{9,7},{10,... | collective-permute-start | bytes 1179656 | tf_op jit(solution)/shard_map/ppermute | solution.py:43
  44.8 1.9 %collective-permute-start.12 = (bf16[160,3072]{1,0:T(8,128)(2,1)S(1)}, bf16[160,3072]{1,0:T(8,128)(2,1)S(1)}, u32[]{:S(2)}, u32[]{:S(2)}) collective-permute-start(bf16[160,3072]{1,0:T(8,128)(2,1)S(1)} %joined.8.refs_4_), channel_id=1, source_target_pairs={{0,1},{1,0},{2,3},{3,2},{4,5},{5,4},{6,7},{7,6},{8,9},{9,8},{10,11... | collective-permute-start | bytes 2949128 | tf_op jit(solution)/shard_map/ppermute | solution.py:39
  46.8 2.4 %collective-permute-start.13 = (bf16[128,3072]{1,0:T(8,128)(2,1)S(1)}, bf16[128,3072]{1,0:T(8,128)(2,1)S(1)}, u32[]{:S(2)}, u32[]{:S(2)}) collective-permute-start(bf16[128,3072]{1,0:T(8,128)(2,1)S(1)} %joined.9.refs_2_), channel_id=1, source_target_pairs={{0,1},{1,0},{2,3},{3,2},{4,5},{5,4},{6,7},{7,6},{8,9},{9,8},{10,11... | collective-permute-start | bytes 2359304 | tf_op jit(solution)/shard_map/ppermute | solution.py:39
  49.3 1.0 collective-permute-done.7.x.refs_1_
  50.3 5.1 %collective-permute-start.10 = (bf16[128,3072]{1,0:T(8,128)(2,1)S(1)}, bf16[128,3072]{1,0:T(8,128)(2,1)S(1)}, u32[]{:S(2)}, u32[]{:S(2)}) collective-permute-start(bf16[128,3072]{1,0:T(8,128)(2,1)S(1)} %joined.7.refs_0_), channel_id=1, source_target_pairs={{0,1},{1,0},{2,3},{3,2},{4,5},{5,4},{6,7},{7,6},{8,9},{9,8},{10,11... | collective-permute-start | bytes 2359304 | tf_op jit(solution)/shard_map/ppermute | solution.py:39
  55.4 2.4 %collective-permute-start.4 = (bf16[32,3072]{1,0:T(8,128)(2,1)S(1)}, bf16[32,3072]{1,0:T(8,128)(2,1)S(1)}, u32[]{:S(2)}, u32[]{:S(2)}) collective-permute-start(bf16[32,3072]{1,0:T(8,128)(2,1)S(1)} %upper.2), channel_id=1, source_target_pairs={{0,2},{1,15},{2,4},{3,1},{4,6},{5,3},{6,8},{7,5},{8,10},{9,7},{10,... | collective-permute-start | bytes 589832 | tf_op jit(solution)/shard_map/ppermute | solution.py:43
  57.9 2.6 %collective-permute-start.8 = (bf16[32,3072]{1,0:T(8,128)(2,1)S(1)}, bf16[32,3072]{1,0:T(8,128)(2,1)S(1)}, u32[]{:S(2)}, u32[]{:S(2)}) collective-permute-start(bf16[32,3072]{1,0:T(8,128)(2,1)S(1)} %upper.3), channel_id=1, source_target_pairs={{0,2},{1,15},{2,4},{3,1},{4,6},{5,3},{6,8},{7,5},{8,10},{9,7},{10,... | collective-permute-start | bytes 589832 | tf_op jit(solution)/shard_map/ppermute | solution.py:43
  60.5 1.7 %collective-permute-done.4.refs_0_ = bf16[32,3072]{1,0:T(8,128)(2,1)S(1)} collective-permute-done((bf16[32,3072]{1,0:T(8,128)(2,1)S(1)}, bf16[32,3072]{1,0:T(8,128)(2,1)S(1)}, u32[]{:S(2)}, u32[]{:S(2)}) %collective-permute-start.4) | collective-permute-done | bytes 196640 | tf_op jit(solution)/shard_map/ppermute | solution.py:43
  62.1 2.5 %collective-permute-done.8.refs_1_ = bf16[32,3072]{1,0:T(8,128)(2,1)S(1)} collective-permute-done((bf16[32,3072]{1,0:T(8,128)(2,1)S(1)}, bf16[32,3072]{1,0:T(8,128)(2,1)S(1)}, u32[]{:S(2)}, u32[]{:S(2)}) %collective-permute-start.8) | collective-permute-done | bytes 196640 | tf_op jit(solution)/shard_map/ppermute | solution.py:43
  64.6 3.6 %collective-permute-start.9 = (bf16[64,3072]{1,0:T(8,128)(2,1)S(1)}, bf16[64,3072]{1,0:T(8,128)(2,1)S(1)}, u32[]{:S(2)}, u32[]{:S(2)}) collective-permute-start(bf16[64,3072]{1,0:T(8,128)(2,1)S(1)} %joined.6.refs_0_), channel_id=1, source_target_pairs={{0,1},{1,0},{2,3},{3,2},{4,5},{5,4},{6,7},{7,6},{8,9},{9,8},{10,11... | collective-permute-start | bytes 1179656 | tf_op jit(solution)/shard_map/ppermute | solution.py:39
  68.3 0.7 fusion.17
  69.0 2.7 %fusion.9.first.refs_1_ = s32[256]{0:T(256)S(1)} fusion(s32[256]{0:T(256)S(1)} %copy-done.1, s32[]{:T(128)} %bitcast.10, s32[]{:T(128)} %bitcast.9, s32[]{:T(128)} %bitcast.8, s32[256]{0:T(256)S(1)} %get-tuple-element.22, s32[]{:T(128)} %bitcast.7), kind=kLoop, calls=%fused_computation.49 | loop fusion | flops 32256 | bytes 3088 | tf_op jit(solution)/shard_map/add | solution.py:312
  71.6 2.5 %product.4 = (f32[1024,512]{1,0:T(8,128)S(1)}, bf16[3072,512]{1,0:T(8,128)(2,1)S(1)}) custom-call(bf16[64,3072]{1,0:T(8,128)(2,1)S(1)} %joined.5.refs_0_, bf16[1024,512]{1,0:T(8,128)(2,1)} %refs_1_.1, bf16[1024,512]{1,0:T(8,128)(2,1)} %refs_2_.1, bf16[1024,512]{1,0:T(8,128)(2,1)} %refs_3_.1), custom_call_target="tpu_custom_call" | custom-call | tf_op jit(solution)/shard_map/product/pallas_call | solution.py:236
  74.2 2.0 %product.5 = (f32[1024,512]{1,0:T(8,128)S(1)}, bf16[3072,512]{1,0:T(8,128)(2,1)S(1)}) custom-call(bf16[32,3072]{1,0:T(8,128)(2,1)S(1)} %collective-permute-done.11.refs_2_.refs_0_, bf16[160,3072]{1,0:T(8,128)(2,1)S(1)} %collective-permute-done.12.refs_1_, bf16[128,3072]{1,0:T(8,128)(2,1)S(1)} %joined.9.refs_2_, ...), custom_call_target="tpu_custom_call", output_to_operand_aliasing={{0}: (6, {}), {1}: (5, {})} | custom-call | tf_op jit(solution)/shard_map/product/pallas_call | solution.py:236
  76.2 1.0 product.6
  77.2 0.6 product.7
  77.8 3.1 %taken.6 = f32[6,96,512]{2,1,0:T(8,128)S(1)} custom-call(s32[7]{0:T(128)S(1)} %stack.31.me.refs_0_, s32[256]{0:T(256)S(1)} %fusion.9.first.refs_1_, s32[256]{0:T(256)S(1)} %get-tuple-element.21.turn.refs_2_, f32[1024,512]{1,0:T(8,128)S(1)} %get-tuple-element.18.values.refs_3_), custom_call_target="tpu_custom_call" | custom-call | tf_op jit(solution)/shard_map/taken/pallas_call | solution.py:112
  80.9 1.9 %collective-permute-start.15 = (f32[6,96,512]{2,1,0:T(8,128)S(1)}, f32[6,96,512]{2,1,0:T(8,128)S(1)}, u32[]{:S(2)}, u32[]{:S(2)}) collective-permute-start(f32[6,96,512]{2,1,0:T(8,128)S(1)} %taken.6), channel_id=1, source_target_pairs={{0,1},{1,0},{2,3},{3,2},{4,5},{5,4},{6,7},{7,6},{8,9},{9,8},{10,11... | collective-permute-start | bytes 3538952 | tf_op jit(solution)/shard_map/ppermute | solution.py:39
  82.8 1.0 taken.7
  83.8 2.4 %collective-permute-start.16 = (f32[1,96,512]{2,1,0:T(8,128)S(1)}, f32[1,96,512]{2,1,0:T(8,128)S(1)}, u32[]{:S(2)}, u32[]{:S(2)}) collective-permute-start(f32[1,96,512]{2,1,0:T(8,128)S(1)} %taken.7), channel_id=1, source_target_pairs={{0,1},{1,0},{2,3},{3,2},{4,5},{5,4},{6,7},{7,6},{8,9},{9,8},{10,11... | collective-permute-start | bytes 589832 | tf_op jit(solution)/shard_map/ppermute | solution.py:39
  86.2 1.0 collective-permute-done.16.refs_4_
  87.3 1.0 paired.7
  88.3 5.1 %collective-permute-start.17 = (f32[2,96,512]{2,1,0:T(8,128)S(1)}, f32[2,96,512]{2,1,0:T(8,128)S(1)}, u32[]{:S(2)}, u32[]{:S(2)}) collective-permute-start(f32[2,96,512]{2,1,0:T(8,128)S(1)} %paired.7), channel_id=1, source_target_pairs={{0,32},{1,225},{32,64},{33,1},{64,96},{65,33},{96,128},{97,65},{12... | collective-permute-start | bytes 1179656 | tf_op jit(solution)/shard_map/ppermute | solution.py:43
  93.4 4.7 %collective-permute-done.17.refs_5_ = f32[2,96,512]{2,1,0:T(8,128)S(1)} collective-permute-done((f32[2,96,512]{2,1,0:T(8,128)S(1)}, f32[2,96,512]{2,1,0:T(8,128)S(1)}, u32[]{:S(2)}, u32[]{:S(2)}) %collective-permute-start.17) | collective-permute-done | bytes 393248 | tf_op jit(solution)/shard_map/ppermute | solution.py:43
  98.1 1.1 paired.8
  99.1 5.0 %collective-permute-start.18 = (f32[2,96,512]{2,1,0:T(8,128)S(1)}, f32[2,96,512]{2,1,0:T(8,128)S(1)}, u32[]{:S(2)}, u32[]{:S(2)}) collective-permute-start(f32[2,96,512]{2,1,0:T(8,128)S(1)} %paired.8), channel_id=1, source_target_pairs={{0,32},{1,225},{32,64},{33,1},{64,96},{65,33},{96,128},{97,65},{12... | collective-permute-start | bytes 1179656 | tf_op jit(solution)/shard_map/ppermute | solution.py:43
  104.2 1.0 paired.11
  105.2 2.1 %collective-permute-start.21 = (f32[2,96,512]{2,1,0:T(8,128)S(1)}, f32[2,96,512]{2,1,0:T(8,128)S(1)}, u32[]{:S(2)}, u32[]{:S(2)}) collective-permute-start(f32[2,96,512]{2,1,0:T(8,128)S(1)} %paired.11), channel_id=1, source_target_pairs={{0,32},{1,225},{32,64},{33,1},{64,96},{65,33},{96,128},{97,65},{12... | collective-permute-start | bytes 1179656 | tf_op jit(solution)/shard_map/ppermute | solution.py:43
  107.3 1.6 collective-permute-done.18.refs_5_
  108.9 1.0 paired.9
  109.9 5.0 %collective-permute-start.19 = (f32[2,96,512]{2,1,0:T(8,128)S(1)}, f32[2,96,512]{2,1,0:T(8,128)S(1)}, u32[]{:S(2)}, u32[]{:S(2)}) collective-permute-start(f32[2,96,512]{2,1,0:T(8,128)S(1)} %paired.9), channel_id=1, source_target_pairs={{0,32},{1,225},{32,64},{33,1},{64,96},{65,33},{96,128},{97,65},{12... | collective-permute-start | bytes 1179656 | tf_op jit(solution)/shard_map/ppermute | solution.py:43
  115.0 1.0 paired.12
  116.0 3.2 %collective-permute-start.22 = (f32[2,96,512]{2,1,0:T(8,128)S(1)}, f32[2,96,512]{2,1,0:T(8,128)S(1)}, u32[]{:S(2)}, u32[]{:S(2)}) collective-permute-start(f32[2,96,512]{2,1,0:T(8,128)S(1)} %paired.12), channel_id=1, source_target_pairs={{0,32},{1,225},{32,64},{33,1},{64,96},{65,33},{96,128},{97,65},{12... | collective-permute-start | bytes 1179656 | tf_op jit(solution)/shard_map/ppermute | solution.py:43
  119.1 0.5 collective-permute-done.19.refs_5_
  119.7 1.0 paired.10
  120.7 7.2 %collective-permute-start.20 = (f32[2,96,512]{2,1,0:T(8,128)S(1)}, f32[2,96,512]{2,1,0:T(8,128)S(1)}, u32[]{:S(2)}, u32[]{:S(2)}) collective-permute-start(f32[2,96,512]{2,1,0:T(8,128)S(1)} %paired.10), channel_id=1, source_target_pairs={{0,288},{1,481},{32,320},{33,257},{64,352},{65,289},{96,384},{97,3... | collective-permute-start | bytes 1179656 | tf_op jit(solution)/shard_map/ppermute | solution.py:332
  127.9 1.0 paired.13
  129.0 1.9 %collective-permute-start.23 = (f32[2,96,512]{2,1,0:T(8,128)S(1)}, f32[2,96,512]{2,1,0:T(8,128)S(1)}, u32[]{:S(2)}, u32[]{:S(2)}) collective-permute-start(f32[2,96,512]{2,1,0:T(8,128)S(1)} %paired.13), channel_id=1, source_target_pairs={{0,32},{1,225},{32,64},{33,1},{64,96},{65,33},{96,128},{97,65},{12... | collective-permute-start | bytes 1179656 | tf_op jit(solution)/shard_map/ppermute | solution.py:43
  130.9 1.0 taken.5
  131.9 3.4 %collective-permute-start.14 = (f32[96,512]{1,0:T(8,128)S(1)}, f32[96,512]{1,0:T(8,128)S(1)}, u32[]{:S(2)}, u32[]{:S(2)}) collective-permute-start(f32[96,512]{1,0:T(8,128)S(1)} %bitcast.34), channel_id=1, source_target_pairs={{0,256},{256,0},{1,257},{257,1},{2,258},{258,2},{3,259},{259,3},{4... | collective-permute-start | bytes 589832 | tf_op jit(solution)/shard_map/ppermute | solution.py:324
  135.3 3.0 %collective-permute-done.23 = f32[2,96,512]{2,1,0:T(8,128)S(1)} collective-permute-done((f32[2,96,512]{2,1,0:T(8,128)S(1)}, f32[2,96,512]{2,1,0:T(8,128)S(1)}, u32[]{:S(2)}, u32[]{:S(2)}) %collective-permute-start.23) | collective-permute-done | bytes 393248 | tf_op jit(solution)/shard_map/ppermute | solution.py:43
  138.3 5.6 %collective-permute-start.24 = (f32[96,512]{1,0:T(8,128)S(1)}, f32[96,512]{1,0:T(8,128)}, u32[]{:S(2)}, u32[]{:S(2)}) collective-permute-start(f32[96,512]{1,0:T(8,128)S(1)} %fusion), channel_id=1, source_target_pairs={{0,1},{1,0},{2,3},{3,2},{4,5},{5,4},{6,7},{7,6},{8,9},{9,8},{10,11... | collective-permute-start | bytes 589832 | tf_op jit(solution)/shard_map/ppermute | solution.py:39
  143.9 0.1 dynamic_slice.3
  144.0 0.2 select_reduce_fusion
  144.2 1.0 taken.4
  145.2 1.1 multiply_reduce_fusion
  146.3 0.6 broadcast_in_dim.45
  146.9 4.0 %all-to-all-start = ((f32[32,1,96]{2,1,0:T(1,128)}), f32[32,1,96]{2,1,0:T(1,128)S(1)}, u32[]{:S(2)}, u32[]{:S(2)}) async-start(f32[32,1,96]{2,1,0:T(1,128)} %broadcast_in_dim.45), calls=%async_computation | async-start | bytes 32768 | tf_op jit(solution)/shard_map/all_to_all | solution.py:340
  151.1 0.1 le.23
  151.2 7.6 %all-to-all-done = f32[32,1,96]{2,1,0:T(1,128)S(1)} async-done(((f32[32,1,96]{2,1,0:T(1,128)}), f32[32,1,96]{2,1,0:T(1,128)S(1)}, u32[]{:S(2)}, u32[]{:S(2)}) %all-to-all-start) | async-done | bytes 12320 | tf_op jit(solution)/shard_map/all_to_all | solution.py:340
  158.8 0.7 select_convert_fusion
  (31 shorter events, 0.5 us)
Async XLA Ops:
  2.0 9.8 %collective-permute-start = (bf16[32,3072]{1,0:T(8,128)(2,1)S(1)}, bf16[32,3072]{1,0:T(8,128)(2,1)S(1)}, u32[]{:S(2)}, u32[]{:S(2)}) collective-permute-start(bf16[32,3072]{1,0:T(8,128)(2,1)S(1)} %pick.1.refs_0_), channel_id=1, source_target_pairs={{0,1},{1,0},{2,3},{3,2},{4,5},{5,4},{6,7},{7,6},{8,9},{9,8},{10,11... | collective-permute-start | bytes 589832 | tf_op jit(solution)/shard_map/ppermute | solution.py:39
  11.8 10.0 %collective-permute-start.1 = (bf16[64,3072]{1,0:T(8,128)(2,1)S(1)}, bf16[64,3072]{1,0:T(8,128)(2,1)S(1)}, u32[]{:S(2)}, u32[]{:S(2)}) collective-permute-start(bf16[64,3072]{1,0:T(8,128)(2,1)S(1)} %joined.5.refs_0_), channel_id=1, source_target_pairs={{0,2},{1,15},{2,4},{3,1},{4,6},{5,3},{6,8},{7,5},{8,10},{9,7},{10,... | collective-permute-start | bytes 1179656 | tf_op jit(solution)/shard_map/ppermute | solution.py:43
  17.2 13.3 %collective-permute-start.5 = (bf16[64,3072]{1,0:T(8,128)(2,1)S(1)}, bf16[64,3072]{1,0:T(8,128)(2,1)S(1)}, u32[]{:S(2)}, u32[]{:S(2)}) collective-permute-start(bf16[64,3072]{1,0:T(8,128)(2,1)S(1)} %joined.5.refs_0_), channel_id=1, source_target_pairs={{0,18},{1,31},{2,20},{3,17},{4,22},{5,19},{6,24},{7,21},{8,26},{9,... | collective-permute-start | bytes 1179656 | tf_op jit(solution)/shard_map/ppermute | solution.py:263
  21.9 15.4 %collective-permute-start.2 = (bf16[64,3072]{1,0:T(8,128)(2,1)S(1)}, bf16[64,3072]{1,0:T(8,128)(2,1)S(1)}, u32[]{:S(2)}, u32[]{:S(2)}) collective-permute-start(bf16[64,3072]{1,0:T(8,128)(2,1)S(1)} %collective-permute-done.1.refs_0_), channel_id=1, source_target_pairs={{0,2},{1,15},{2,4},{3,1},{4,6},{5,3},{6,8},{7,5},{8,10},{9,7},{10,... | collective-permute-start | bytes 1179656 | tf_op jit(solution)/shard_map/ppermute | solution.py:43
  30.4 9.3 %collective-permute-start.6 = (bf16[64,3072]{1,0:T(8,128)(2,1)S(1)}, bf16[64,3072]{1,0:T(8,128)(2,1)S(1)}, u32[]{:S(2)}, u32[]{:S(2)}) collective-permute-start(bf16[64,3072]{1,0:T(8,128)(2,1)S(1)} %collective-permute-done.5.refs_1_), channel_id=1, source_target_pairs={{0,2},{1,15},{2,4},{3,1},{4,6},{5,3},{6,8},{7,5},{8,10},{9,7},{10,... | collective-permute-start | bytes 1179656 | tf_op jit(solution)/shard_map/ppermute | solution.py:43
  35.0 9.7 %collective-permute-start.11 = (bf16[32,3072]{1,0:T(8,128)(2,1)S(1)}, bf16[32,3072]{1,0:T(8,128)(2,1)S(1)}, u32[]{:S(2)}, u32[]{:S(2)}) collective-permute-start(bf16[32,3072]{1,0:T(8,128)(2,1)S(1)} %pick.1.refs_0_), channel_id=1, source_target_pairs={{0,16},{16,0},{1,17},{17,1},{2,18},{18,2},{3,19},{19,3},{4,20},{20... | collective-permute-start | bytes 589832 | tf_op jit(solution)/shard_map/ppermute | solution.py:264
  37.2 12.0 %collective-permute-start.3 = (bf16[64,3072]{1,0:T(8,128)(2,1)S(1)}, bf16[64,3072]{1,0:T(8,128)(2,1)S(1)}, u32[]{:S(2)}, u32[]{:S(2)}) collective-permute-start(bf16[64,3072]{1,0:T(8,128)(2,1)S(1)} %collective-permute-done.2.refs_0_), channel_id=1, source_target_pairs={{0,2},{1,15},{2,4},{3,1},{4,6},{5,3},{6,8},{7,5},{8,10},{9,7},{10,... | collective-permute-start | bytes 1179656 | tf_op jit(solution)/shard_map/ppermute | solution.py:43
  39.7 10.5 %collective-permute-start.7 = (bf16[64,3072]{1,0:T(8,128)(2,1)S(1)}, bf16[64,3072]{1,0:T(8,128)(2,1)S(1)}, u32[]{:S(2)}, u32[]{:S(2)}) collective-permute-start(bf16[64,3072]{1,0:T(8,128)(2,1)S(1)} %collective-permute-done.6.refs_1_), channel_id=1, source_target_pairs={{0,2},{1,15},{2,4},{3,1},{4,6},{5,3},{6,8},{7,5},{8,10},{9,7},{10,... | collective-permute-start | bytes 1179656 | tf_op jit(solution)/shard_map/ppermute | solution.py:43
  44.8 29.4 %collective-permute-start.12 = (bf16[160,3072]{1,0:T(8,128)(2,1)S(1)}, bf16[160,3072]{1,0:T(8,128)(2,1)S(1)}, u32[]{:S(2)}, u32[]{:S(2)}) collective-permute-start(bf16[160,3072]{1,0:T(8,128)(2,1)S(1)} %joined.8.refs_4_), channel_id=1, source_target_pairs={{0,1},{1,0},{2,3},{3,2},{4,5},{5,4},{6,7},{7,6},{8,9},{9,8},{10,11... | collective-permute-start | bytes 2949128 | tf_op jit(solution)/shard_map/ppermute | solution.py:39
  46.8 21.4 %copy-start.1 = (s32[256]{0:T(256)S(1)}, s32[256]{0:T(256)}, u32[]{:S(2)}) copy-start(s32[256]{0:T(256)} %param.17) | copy-start | bytes 3076
  46.8 27.4 %collective-permute-start.13 = (bf16[128,3072]{1,0:T(8,128)(2,1)S(1)}, bf16[128,3072]{1,0:T(8,128)(2,1)S(1)}, u32[]{:S(2)}, u32[]{:S(2)}) collective-permute-start(bf16[128,3072]{1,0:T(8,128)(2,1)S(1)} %joined.9.refs_2_), channel_id=1, source_target_pairs={{0,1},{1,0},{2,3},{3,2},{4,5},{5,4},{6,7},{7,6},{8,9},{9,8},{10,11... | collective-permute-start | bytes 2359304 | tf_op jit(solution)/shard_map/ppermute | solution.py:39
  50.3 25.9 %collective-permute-start.10 = (bf16[128,3072]{1,0:T(8,128)(2,1)S(1)}, bf16[128,3072]{1,0:T(8,128)(2,1)S(1)}, u32[]{:S(2)}, u32[]{:S(2)}) collective-permute-start(bf16[128,3072]{1,0:T(8,128)(2,1)S(1)} %joined.7.refs_0_), channel_id=1, source_target_pairs={{0,1},{1,0},{2,3},{3,2},{4,5},{5,4},{6,7},{7,6},{8,9},{9,8},{10,11... | collective-permute-start | bytes 2359304 | tf_op jit(solution)/shard_map/ppermute | solution.py:39
  55.4 6.7 %collective-permute-start.4 = (bf16[32,3072]{1,0:T(8,128)(2,1)S(1)}, bf16[32,3072]{1,0:T(8,128)(2,1)S(1)}, u32[]{:S(2)}, u32[]{:S(2)}) collective-permute-start(bf16[32,3072]{1,0:T(8,128)(2,1)S(1)} %upper.2), channel_id=1, source_target_pairs={{0,2},{1,15},{2,4},{3,1},{4,6},{5,3},{6,8},{7,5},{8,10},{9,7},{10,... | collective-permute-start | bytes 589832 | tf_op jit(solution)/shard_map/ppermute | solution.py:43
  57.9 6.7 %collective-permute-start.8 = (bf16[32,3072]{1,0:T(8,128)(2,1)S(1)}, bf16[32,3072]{1,0:T(8,128)(2,1)S(1)}, u32[]{:S(2)}, u32[]{:S(2)}) collective-permute-start(bf16[32,3072]{1,0:T(8,128)(2,1)S(1)} %upper.3), channel_id=1, source_target_pairs={{0,2},{1,15},{2,4},{3,1},{4,6},{5,3},{6,8},{7,5},{8,10},{9,7},{10,... | collective-permute-start | bytes 589832 | tf_op jit(solution)/shard_map/ppermute | solution.py:43
  64.6 12.6 %collective-permute-start.9 = (bf16[64,3072]{1,0:T(8,128)(2,1)S(1)}, bf16[64,3072]{1,0:T(8,128)(2,1)S(1)}, u32[]{:S(2)}, u32[]{:S(2)}) collective-permute-start(bf16[64,3072]{1,0:T(8,128)(2,1)S(1)} %joined.6.refs_0_), channel_id=1, source_target_pairs={{0,1},{1,0},{2,3},{3,2},{4,5},{5,4},{6,7},{7,6},{8,9},{9,8},{10,11... | collective-permute-start | bytes 1179656 | tf_op jit(solution)/shard_map/ppermute | solution.py:39
  80.9 17.2 %collective-permute-start.15 = (f32[6,96,512]{2,1,0:T(8,128)S(1)}, f32[6,96,512]{2,1,0:T(8,128)S(1)}, u32[]{:S(2)}, u32[]{:S(2)}) collective-permute-start(f32[6,96,512]{2,1,0:T(8,128)S(1)} %taken.6), channel_id=1, source_target_pairs={{0,1},{1,0},{2,3},{3,2},{4,5},{5,4},{6,7},{7,6},{8,9},{9,8},{10,11... | collective-permute-start | bytes 3538952 | tf_op jit(solution)/shard_map/ppermute | solution.py:39
  83.8 3.5 %collective-permute-start.16 = (f32[1,96,512]{2,1,0:T(8,128)S(1)}, f32[1,96,512]{2,1,0:T(8,128)S(1)}, u32[]{:S(2)}, u32[]{:S(2)}) collective-permute-start(f32[1,96,512]{2,1,0:T(8,128)S(1)} %taken.7), channel_id=1, source_target_pairs={{0,1},{1,0},{2,3},{3,2},{4,5},{5,4},{6,7},{7,6},{8,9},{9,8},{10,11... | collective-permute-start | bytes 589832 | tf_op jit(solution)/shard_map/ppermute | solution.py:39
  88.3 9.8 %collective-permute-start.17 = (f32[2,96,512]{2,1,0:T(8,128)S(1)}, f32[2,96,512]{2,1,0:T(8,128)S(1)}, u32[]{:S(2)}, u32[]{:S(2)}) collective-permute-start(f32[2,96,512]{2,1,0:T(8,128)S(1)} %paired.7), channel_id=1, source_target_pairs={{0,32},{1,225},{32,64},{33,1},{64,96},{65,33},{96,128},{97,65},{12... | collective-permute-start | bytes 1179656 | tf_op jit(solution)/shard_map/ppermute | solution.py:43
  99.1 9.7 %collective-permute-start.18 = (f32[2,96,512]{2,1,0:T(8,128)S(1)}, f32[2,96,512]{2,1,0:T(8,128)S(1)}, u32[]{:S(2)}, u32[]{:S(2)}) collective-permute-start(f32[2,96,512]{2,1,0:T(8,128)S(1)} %paired.8), channel_id=1, source_target_pairs={{0,32},{1,225},{32,64},{33,1},{64,96},{65,33},{96,128},{97,65},{12... | collective-permute-start | bytes 1179656 | tf_op jit(solution)/shard_map/ppermute | solution.py:43
  105.2 9.7 %collective-permute-start.21 = (f32[2,96,512]{2,1,0:T(8,128)S(1)}, f32[2,96,512]{2,1,0:T(8,128)S(1)}, u32[]{:S(2)}, u32[]{:S(2)}) collective-permute-start(f32[2,96,512]{2,1,0:T(8,128)S(1)} %paired.11), channel_id=1, source_target_pairs={{0,32},{1,225},{32,64},{33,1},{64,96},{65,33},{96,128},{97,65},{12... | collective-permute-start | bytes 1179656 | tf_op jit(solution)/shard_map/ppermute | solution.py:43
  109.9 9.7 %collective-permute-start.19 = (f32[2,96,512]{2,1,0:T(8,128)S(1)}, f32[2,96,512]{2,1,0:T(8,128)S(1)}, u32[]{:S(2)}, u32[]{:S(2)}) collective-permute-start(f32[2,96,512]{2,1,0:T(8,128)S(1)} %paired.9), channel_id=1, source_target_pairs={{0,32},{1,225},{32,64},{33,1},{64,96},{65,33},{96,128},{97,65},{12... | collective-permute-start | bytes 1179656 | tf_op jit(solution)/shard_map/ppermute | solution.py:43
  116.0 11.9 %collective-permute-start.22 = (f32[2,96,512]{2,1,0:T(8,128)S(1)}, f32[2,96,512]{2,1,0:T(8,128)S(1)}, u32[]{:S(2)}, u32[]{:S(2)}) collective-permute-start(f32[2,96,512]{2,1,0:T(8,128)S(1)} %paired.12), channel_id=1, source_target_pairs={{0,32},{1,225},{32,64},{33,1},{64,96},{65,33},{96,128},{97,65},{12... | collective-permute-start | bytes 1179656 | tf_op jit(solution)/shard_map/ppermute | solution.py:43
  120.7 14.6 %collective-permute-start.20 = (f32[2,96,512]{2,1,0:T(8,128)S(1)}, f32[2,96,512]{2,1,0:T(8,128)S(1)}, u32[]{:S(2)}, u32[]{:S(2)}) collective-permute-start(f32[2,96,512]{2,1,0:T(8,128)S(1)} %paired.10), channel_id=1, source_target_pairs={{0,288},{1,481},{32,320},{33,257},{64,352},{65,289},{96,384},{97,3... | collective-permute-start | bytes 1179656 | tf_op jit(solution)/shard_map/ppermute | solution.py:332
  128.9 15.1 %copy-start = (s32[256]{0:T(256)S(1)}, s32[256]{0:T(256)}, u32[]{:S(2)}) copy-start(s32[256]{0:T(256)} %accepted.1) | copy-start | bytes 3076
  129.0 9.3 %collective-permute-start.23 = (f32[2,96,512]{2,1,0:T(8,128)S(1)}, f32[2,96,512]{2,1,0:T(8,128)S(1)}, u32[]{:S(2)}, u32[]{:S(2)}) collective-permute-start(f32[2,96,512]{2,1,0:T(8,128)S(1)} %paired.13), channel_id=1, source_target_pairs={{0,32},{1,225},{32,64},{33,1},{64,96},{65,33},{96,128},{97,65},{12... | collective-permute-start | bytes 1179656 | tf_op jit(solution)/shard_map/ppermute | solution.py:43
  131.9 26.9 %copy-start.2 = (f32[512]{0:T(512)S(1)}, f32[512]{0:T(512)}, u32[]{:S(2)}) copy-start(f32[512]{0:T(512)} %param.15) | copy-start | bytes 6148
  131.9 13.3 %collective-permute-start.14 = (f32[96,512]{1,0:T(8,128)S(1)}, f32[96,512]{1,0:T(8,128)S(1)}, u32[]{:S(2)}, u32[]{:S(2)}) collective-permute-start(f32[96,512]{1,0:T(8,128)S(1)} %bitcast.34), channel_id=1, source_target_pairs={{0,256},{256,0},{1,257},{257,1},{2,258},{258,2},{3,259},{259,3},{4... | collective-permute-start | bytes 589832 | tf_op jit(solution)/shard_map/ppermute | solution.py:324
  138.3 6.9 %collective-permute-start.24 = (f32[96,512]{1,0:T(8,128)S(1)}, f32[96,512]{1,0:T(8,128)}, u32[]{:S(2)}, u32[]{:S(2)}) collective-permute-start(f32[96,512]{1,0:T(8,128)S(1)} %fusion), channel_id=1, source_target_pairs={{0,1},{1,0},{2,3},{3,2},{4,5},{5,4},{6,7},{7,6},{8,9},{9,8},{10,11... | collective-permute-start | bytes 589832 | tf_op jit(solution)/shard_map/ppermute | solution.py:39
  146.9 11.8 %all-to-all-start = ((f32[32,1,96]{2,1,0:T(1,128)}), f32[32,1,96]{2,1,0:T(1,128)S(1)}, u32[]{:S(2)}, u32[]{:S(2)}) async-start(f32[32,1,96]{2,1,0:T(1,128)} %broadcast_in_dim.45), calls=%async_computation | async-start | bytes 32768 | tf_op jit(solution)/shard_map/all_to_all | solution.py:340

commit v2 on v1

--- a/solution.py
+++ b/solution.py
@@ -65,20 +65,6 @@
         compiler_params=SMALL,
         name="joined",
     )(*parts)
-
-
-def upper(x, rows):
-    def kernel(x, out):
-        out[...] = x[:rows]
-
-    return pl.pallas_call(
-        kernel,
-        out_shape=jax.ShapeDtypeStruct((rows, x.shape[1]), x.dtype),
-        in_specs=[VMEM],
-        out_specs=VMEM,
-        compiler_params=SMALL,
-        name="upper",
-    )(x)
 
 
 def each_row(me, first, turn, values, block, do):
@@ -252,9 +238,9 @@
     weights = (w_low, w_mid, w_high)
     xh, y, xl, z, c = (lax.axis_index(a) for a in ("xh", "y", "xl", "z", "c"))
     ny, nz = lax.axis_size("y"), lax.axis_size("z")
-    way = 1 - 2 * c
+    back = 2 * c - 1
     group = (xl * nz + z) * 2 + c
-    me = lax.optimization_barrier(jnp.stack([xh, y, c, group, xl, z, way]))
+    me = jnp.stack([xh, y, c, group, back])
     mine = selected((low_feats, mid_feats, high_feats), me, accepted)
     block = mine.shape[0]
 
@@ -265,12 +251,10 @@
     for _ in range(2):
         straight.append(onward(straight[-1], "z"))
         crossed.append(onward(crossed[-1], "z"))
-    half = upper(straight[-1], block)
-    straight.append(onward(half, "z"))
-    half = upper(crossed[-1], block)
-    crossed.append(onward(half, "z"))
+    straight.append(onward(straight[-1], "z"))
+    crossed.append(onward(crossed[-1], "z"))
     here, there = [], []
-    for s in range(4):
+    for s in range(3):
         here.append(joined(straight[s], crossed[s], *((beside,) if s == 1 else ())))
         there.append(other_core(here[s]))
     cut = 4 * block
@@ -287,15 +271,15 @@
     partial_value, near = product(parts, (near,), total, 2 * block, partial_value)
     parts = [(here[2], 0, cut), (there[2], 0, cut)]
     partial_value, near = product(parts, (near,), total, 20 * block, partial_value)
-    parts = [(here[3], 0, 2 * block), (there[3], 0, 2 * block)]
+    parts = [(straight[3], 0, 2 * block), (crossed[3], 0, 2 * block)]
     partial_value, near = product(parts, (near,), total, 28 * block, partial_value)
 
     per_slab = assignment.shape[0] // (2 * ny)
     target = assignment
     of_group = target // ROWS_G
     there_c, there_z, there_x = of_group % 2, (of_group // 2) % nz, of_group // (2 * nz)
-    dx, dc, dz = there_x ^ me[4], there_c ^ me[2], (there_z - me[5]) % nz
-    step = (nz - me[6] * dz) % nz
+    dx, dc, dz = there_x ^ xl, there_c ^ c, (there_z - z) % nz
+    step = (nz + back * dz) % nz
     near = jnp.minimum(step, nz - step)
     from_here = step < nz // 2
     place = jnp.where(
@@ -303,7 +287,7 @@
         dx * 2 + dc,
         jnp.where(
             near == nz // 2,
-            28 + dc * 2 + dx,
+            28 + dx * 2 + dc,
             near * 8 - 4 + jnp.where(from_here, dx * 2 + dc, 5 + dx * 2 - dc),
         ),
     )

time: 160 us -> 153 us (0.956)
  other arithmetic: 4.84 us -> 2.23 us
  starting transfers between devices: 101 us -> 98.5 us
    add x1, other arithmetic: 2.67 us -> 0.06 us  [step_on_device(): place * block + in_group // 2 * SLOTS + jnp.where(even, 0, SLOTS - 1)]
    ppermute x8 -> x7, starting transfers between devices: 31.7 us -> 29.4 us  [other_core(): return lax.ppermute(x, 'c', SWAP)]
    ppermute x13, waiting for transfers between devices: 17 us -> 15.2 us  [onward(): return lax.ppermute(x, (axis, 'c'), both_ways(lax.axis_size(axis)))]
  transfers between devices with their start and end apart: 26 -> 25, of which waited for: 13 -> 12; matrix products, arithmetic and copies ran while one was open for 2% -> 0% of each run, Pallas kernels for 9% -> 10%
where the time goes in v2:
time: 153 us; the launch traced here: 152 us
  starting transfers between devices  98.5 us (64%)
  waiting for transfers between devices  28.9 us (19%)
  Pallas kernels  21.4 us (14%)
  other arithmetic  2.23 us (1%)
    ppermute x13, starting transfers between devices, onward(): return lax.ppermute(x, (axis, 'c'), both_ways(lax.axis_size(axis)))  49.1 us
    ppermute x7, starting transfers between devices, other_core(): return lax.ppermute(x, 'c', SWAP)  29.4 us
    ppermute x13, waiting for transfers between devices, onward(): return lax.ppermute(x, (axis, 'c'), both_ways(lax.axis_size(axis)))  15.2 us
    all_to_all x1, waiting for transfers between devices, step_on_device(): lax.all_to_all(jnp.broadcast_to(squares[None], (4 * nz, size)), GRP, 0, 0...  7.61 us
    pallas_call x7, Pallas kernels, paired(): pl.pallas_call(kernel, out_shape=jax.ShapeDtypeStruct((2, *theirs.shape[1...  7.22 us
    ppermute x1, starting transfers between devices, step_on_device(): came[v] = lax.ppermute(total, (*TP, 'c'), diagonal(ny))  7.21 us
    pallas_call x4, Pallas kernels, product(): pl.pallas_call(kernel, out_shape=shapes, in_specs=[VMEM] * len(arrays) +...  6.11 us
    pallas_call x4, Pallas kernels, taken(): pl.pallas_call(kernel, out_shape=jax.ShapeDtypeStruct((len(blocks), first...  6.02 us
  transfers between devices with their start and end apart: 25, of which 12 were waited for; matrix products, arithmetic and copies ran while one was open for 0% of the time, Pallas kernels for 10%

profile of v2, /device:TPU:1, one launch (start us, length us, event | category | flops | bytes accessed | tf_op | source)
XLA Modules:
  0.0 152.5 jit_solution(2340572728765865357)
XLA Ops:
  0.0 0.1 stack.23.me.refs_0_
  0.1 1.9 %pick.1.refs_0_ = bf16[32,3072]{1,0:T(8,128)(2,1)S(1)} custom-call(s32[5]{0:T(128)S(1)} %stack.23.me.refs_0_, s32[256]{0:T(256)} %accepted.1, bf16[48,1024]{1,0:T(8,128)(2,1)} %low.1, bf16[48,1024]{1,0:T(8,128)(2,1)} %mid.1, bf16[48,1024]{1,0:T(8,128)(2,1)} %high.1), custom_call_target="tpu_custom_call" | custom-call | tf_op jit(solution)/shard_map/pick/pallas_call | solution.py:165
  2.0 8.7 %collective-permute-start = (bf16[32,3072]{1,0:T(8,128)(2,1)S(1)}, bf16[32,3072]{1,0:T(8,128)(2,1)S(1)}, u32[]{:S(2)}, u32[]{:S(2)}) collective-permute-start(bf16[32,3072]{1,0:T(8,128)(2,1)S(1)} %pick.1.refs_0_), channel_id=1, source_target_pairs={{0,1},{1,0},{2,3},{3,2},{4,5},{5,4},{6,7},{7,6},{8,9},{9,8},{10,11... | collective-permute-start | bytes 589832 | tf_op jit(solution)/shard_map/ppermute | solution.py:39
  10.7 1.0 collective-permute-done.refs_1_
  11.8 5.3 %collective-permute-start.1 = (bf16[64,3072]{1,0:T(8,128)(2,1)S(1)}, bf16[64,3072]{1,0:T(8,128)(2,1)S(1)}, u32[]{:S(2)}, u32[]{:S(2)}) collective-permute-start(bf16[64,3072]{1,0:T(8,128)(2,1)S(1)} %joined.4.refs_0_), channel_id=1, source_target_pairs={{0,2},{1,15},{2,4},{3,1},{4,6},{5,3},{6,8},{7,5},{8,10},{9,7},{10,... | collective-permute-start | bytes 1179656 | tf_op jit(solution)/shard_map/ppermute | solution.py:43
  17.2 3.1 %collective-permute-start.5 = (bf16[64,3072]{1,0:T(8,128)(2,1)S(1)}, bf16[64,3072]{1,0:T(8,128)(2,1)S(1)}, u32[]{:S(2)}, u32[]{:S(2)}) collective-permute-start(bf16[64,3072]{1,0:T(8,128)(2,1)S(1)} %joined.4.refs_0_), channel_id=1, source_target_pairs={{0,18},{1,31},{2,20},{3,17},{4,22},{5,19},{6,24},{7,21},{8,26},{9,... | collective-permute-start | bytes 1179656 | tf_op jit(solution)/shard_map/ppermute | solution.py:249
  20.3 1.6 %collective-permute-done.1.refs_0_ = bf16[64,3072]{1,0:T(8,128)(2,1)S(1)} collective-permute-done((bf16[64,3072]{1,0:T(8,128)(2,1)S(1)}, bf16[64,3072]{1,0:T(8,128)(2,1)S(1)}, u32[]{:S(2)}, u32[]{:S(2)}) %collective-permute-start.1) | collective-permute-done | bytes 393248 | tf_op jit(solution)/shard_map/ppermute | solution.py:43
  21.9 5.0 %collective-permute-start.2 = (bf16[64,3072]{1,0:T(8,128)(2,1)S(1)}, bf16[64,3072]{1,0:T(8,128)(2,1)S(1)}, u32[]{:S(2)}, u32[]{:S(2)}) collective-permute-start(bf16[64,3072]{1,0:T(8,128)(2,1)S(1)} %collective-permute-done.1.refs_0_), channel_id=1, source_target_pairs={{0,2},{1,15},{2,4},{3,1},{4,6},{5,3},{6,8},{7,5},{8,10},{9,7},{10,... | collective-permute-start | bytes 1179656 | tf_op jit(solution)/shard_map/ppermute | solution.py:43
  26.9 3.6 %collective-permute-done.5.refs_1_ = bf16[64,3072]{1,0:T(8,128)(2,1)S(1)} collective-permute-done((bf16[64,3072]{1,0:T(8,128)(2,1)S(1)}, bf16[64,3072]{1,0:T(8,128)(2,1)S(1)}, u32[]{:S(2)}, u32[]{:S(2)}) %collective-permute-start.5) | collective-permute-done | bytes 393248 | tf_op jit(solution)/shard_map/ppermute | solution.py:249
  30.5 4.6 %collective-permute-start.6 = (bf16[64,3072]{1,0:T(8,128)(2,1)S(1)}, bf16[64,3072]{1,0:T(8,128)(2,1)S(1)}, u32[]{:S(2)}, u32[]{:S(2)}) collective-permute-start(bf16[64,3072]{1,0:T(8,128)(2,1)S(1)} %collective-permute-done.5.refs_1_), channel_id=1, source_target_pairs={{0,2},{1,15},{2,4},{3,1},{4,6},{5,3},{6,8},{7,5},{8,10},{9,7},{10,... | collective-permute-start | bytes 1179656 | tf_op jit(solution)/shard_map/ppermute | solution.py:43
  35.0 2.2 %collective-permute-start.10 = (bf16[32,3072]{1,0:T(8,128)(2,1)S(1)}, bf16[32,3072]{1,0:T(8,128)(2,1)S(1)}, u32[]{:S(2)}, u32[]{:S(2)}) collective-permute-start(bf16[32,3072]{1,0:T(8,128)(2,1)S(1)} %pick.1.refs_0_), channel_id=1, source_target_pairs={{0,16},{16,0},{1,17},{17,1},{2,18},{18,2},{3,19},{19,3},{4,20},{20... | collective-permute-start | bytes 589832 | tf_op jit(solution)/shard_map/ppermute | solution.py:250
  37.2 1.9 %collective-permute-start.3 = (bf16[64,3072]{1,0:T(8,128)(2,1)S(1)}, bf16[64,3072]{1,0:T(8,128)(2,1)S(1)}, u32[]{:S(2)}, u32[]{:S(2)}) collective-permute-start(bf16[64,3072]{1,0:T(8,128)(2,1)S(1)} %collective-permute-done.2.refs_0_), channel_id=1, source_target_pairs={{0,2},{1,15},{2,4},{3,1},{4,6},{5,3},{6,8},{7,5},{8,10},{9,7},{10,... | collective-permute-start | bytes 1179656 | tf_op jit(solution)/shard_map/ppermute | solution.py:43
  39.2 0.6 collective-permute-done.6.refs_1_
  39.7 5.0 %collective-permute-start.7 = (bf16[64,3072]{1,0:T(8,128)(2,1)S(1)}, bf16[64,3072]{1,0:T(8,128)(2,1)S(1)}, u32[]{:S(2)}, u32[]{:S(2)}) collective-permute-start(bf16[64,3072]{1,0:T(8,128)(2,1)S(1)} %collective-permute-done.6.refs_1_), channel_id=1, source_target_pairs={{0,2},{1,15},{2,4},{3,1},{4,6},{5,3},{6,8},{7,5},{8,10},{9,7},{10,... | collective-permute-start | bytes 1179656 | tf_op jit(solution)/shard_map/ppermute | solution.py:43
  44.8 0.1 joined.6.refs_4_
  44.8 1.9 %collective-permute-start.11 = (bf16[160,3072]{1,0:T(8,128)(2,1)S(1)}, bf16[160,3072]{1,0:T(8,128)(2,1)S(1)}, u32[]{:S(2)}, u32[]{:S(2)}) collective-permute-start(bf16[160,3072]{1,0:T(8,128)(2,1)S(1)} %joined.6.refs_4_), channel_id=1, source_target_pairs={{0,1},{1,0},{2,3},{3,2},{4,5},{5,4},{6,7},{7,6},{8,9},{9,8},{10,11... | collective-permute-start | bytes 2949128 | tf_op jit(solution)/shard_map/ppermute | solution.py:39
  46.8 0.1 joined.7.refs_2_
  46.8 2.4 %collective-permute-start.12 = (bf16[128,3072]{1,0:T(8,128)(2,1)S(1)}, bf16[128,3072]{1,0:T(8,128)(2,1)S(1)}, u32[]{:S(2)}, u32[]{:S(2)}) collective-permute-start(bf16[128,3072]{1,0:T(8,128)(2,1)S(1)} %joined.7.refs_2_), channel_id=1, source_target_pairs={{0,1},{1,0},{2,3},{3,2},{4,5},{5,4},{6,7},{7,6},{8,9},{9,8},{10,11... | collective-permute-start | bytes 2359304 | tf_op jit(solution)/shard_map/ppermute | solution.py:39
  49.3 1.0 collective-permute-done.7.refs_1_
  50.3 5.1 %collective-permute-start.9 = (bf16[128,3072]{1,0:T(8,128)(2,1)S(1)}, bf16[128,3072]{1,0:T(8,128)(2,1)S(1)}, u32[]{:S(2)}, u32[]{:S(2)}) collective-permute-start(bf16[128,3072]{1,0:T(8,128)(2,1)S(1)} %joined.5.refs_0_), channel_id=1, source_target_pairs={{0,1},{1,0},{2,3},{3,2},{4,5},{5,4},{6,7},{7,6},{8,9},{9,8},{10,11... | collective-permute-start | bytes 2359304 | tf_op jit(solution)/shard_map/ppermute | solution.py:39
  55.4 2.4 %collective-permute-start.4 = (bf16[64,3072]{1,0:T(8,128)(2,1)S(1)}, bf16[64,3072]{1,0:T(8,128)(2,1)S(1)}, u32[]{:S(2)}, u32[]{:S(2)}) collective-permute-start(bf16[64,3072]{1,0:T(8,128)(2,1)S(1)} %collective-permute-done.3.refs_0_), channel_id=1, source_target_pairs={{0,2},{1,15},{2,4},{3,1},{4,6},{5,3},{6,8},{7,5},{8,10},{9,7},{10,... | collective-permute-start | bytes 1179656 | tf_op jit(solution)/shard_map/ppermute | solution.py:43
  57.8 2.6 %collective-permute-start.8 = (bf16[64,3072]{1,0:T(8,128)(2,1)S(1)}, bf16[64,3072]{1,0:T(8,128)(2,1)S(1)}, u32[]{:S(2)}, u32[]{:S(2)}) collective-permute-start(bf16[64,3072]{1,0:T(8,128)(2,1)S(1)} %collective-permute-done.7.refs_1_), channel_id=1, source_target_pairs={{0,2},{1,15},{2,4},{3,1},{4,6},{5,3},{6,8},{7,5},{8,10},{9,7},{10,... | collective-permute-start | bytes 1179656 | tf_op jit(solution)/shard_map/ppermute | solution.py:43
  60.5 0.1 fusion.9.first.refs_1_
  60.5 2.5 %product.4 = (f32[1024,512]{1,0:T(8,128)S(1)}, bf16[3072,512]{1,0:T(8,128)(2,1)S(1)}) custom-call(bf16[64,3072]{1,0:T(8,128)(2,1)S(1)} %joined.4.refs_0_, bf16[1024,512]{1,0:T(8,128)(2,1)} %refs_1_.1, bf16[1024,512]{1,0:T(8,128)(2,1)} %refs_2_.1, bf16[1024,512]{1,0:T(8,128)(2,1)} %refs_3_.1), custom_call_target="tpu_custom_call" | custom-call | tf_op jit(solution)/shard_map/product/pallas_call | solution.py:222
  63.1 2.0 %product.5 = (f32[1024,512]{1,0:T(8,128)S(1)}, bf16[3072,512]{1,0:T(8,128)(2,1)S(1)}) custom-call(bf16[32,3072]{1,0:T(8,128)(2,1)S(1)} %collective-permute-done.10.refs_2_.refs_0_, bf16[160,3072]{1,0:T(8,128)(2,1)S(1)} %collective-permute-done.11.refs_1_, bf16[128,3072]{1,0:T(8,128)(2,1)S(1)} %joined.7.refs_2_, ...), custom_call_target="tpu_custom_call", output_to_operand_aliasing={{0}: (6, {}), {1}: (5, {})} | custom-call | tf_op jit(solution)/shard_map/product/pallas_call | solution.py:222
  65.1 1.0 product.6
  66.1 2.3 %collective-permute-done.8.refs_1_ = bf16[64,3072]{1,0:T(8,128)(2,1)S(1)} collective-permute-done((bf16[64,3072]{1,0:T(8,128)(2,1)S(1)}, bf16[64,3072]{1,0:T(8,128)(2,1)S(1)}, u32[]{:S(2)}, u32[]{:S(2)}) %collective-permute-start.8) | collective-permute-done | bytes 393248 | tf_op jit(solution)/shard_map/ppermute | solution.py:43
  68.4 0.6 product.7
  69.0 3.1 %taken.6 = f32[6,96,512]{2,1,0:T(8,128)S(1)} custom-call(s32[5]{0:T(128)S(1)} %stack.23.me.refs_0_, s32[256]{0:T(256)S(1)} %fusion.9.first.refs_1_, s32[256]{0:T(256)S(1)} %get-tuple-element.21.turn.refs_2_, f32[1024,512]{1,0:T(8,128)S(1)} %get-tuple-element.18.values.refs_3_), custom_call_target="tpu_custom_call" | custom-call | tf_op jit(solution)/shard_map/taken/pallas_call | solution.py:98
  72.1 4.0 %collective-permute-start.14 = (f32[6,96,512]{2,1,0:T(8,128)S(1)}, f32[6,96,512]{2,1,0:T(8,128)S(1)}, u32[]{:S(2)}, u32[]{:S(2)}) collective-permute-start(f32[6,96,512]{2,1,0:T(8,128)S(1)} %taken.6), channel_id=1, source_target_pairs={{0,1},{1,0},{2,3},{3,2},{4,5},{5,4},{6,7},{7,6},{8,9},{9,8},{10,11... | collective-permute-start | bytes 3538952 | tf_op jit(solution)/shard_map/ppermute | solution.py:39
  76.1 1.0 taken.7
  77.1 1.9 %collective-permute-start.15 = (f32[1,96,512]{2,1,0:T(8,128)S(1)}, f32[1,96,512]{2,1,0:T(8,128)S(1)}, u32[]{:S(2)}, u32[]{:S(2)}) collective-permute-start(f32[1,96,512]{2,1,0:T(8,128)S(1)} %taken.7), channel_id=1, source_target_pairs={{0,1},{1,0},{2,3},{3,2},{4,5},{5,4},{6,7},{7,6},{8,9},{9,8},{10,11... | collective-permute-start | bytes 589832 | tf_op jit(solution)/shard_map/ppermute | solution.py:39
  79.0 1.4 collective-permute-done.15.refs_4_
  80.4 1.0 paired.7
  81.4 5.1 %collective-permute-start.16 = (f32[2,96,512]{2,1,0:T(8,128)S(1)}, f32[2,96,512]{2,1,0:T(8,128)S(1)}, u32[]{:S(2)}, u32[]{:S(2)}) collective-permute-start(f32[2,96,512]{2,1,0:T(8,128)S(1)} %paired.7), channel_id=1, source_target_pairs={{0,32},{1,225},{32,64},{33,1},{64,96},{65,33},{96,128},{97,65},{12... | collective-permute-start | bytes 1179656 | tf_op jit(solution)/shard_map/ppermute | solution.py:43
  86.5 4.7 %collective-permute-done.16.refs_5_ = f32[2,96,512]{2,1,0:T(8,128)S(1)} collective-permute-done((f32[2,96,512]{2,1,0:T(8,128)S(1)}, f32[2,96,512]{2,1,0:T(8,128)S(1)}, u32[]{:S(2)}, u32[]{:S(2)}) %collective-permute-start.16) | collective-permute-done | bytes 393248 | tf_op jit(solution)/shard_map/ppermute | solution.py:43
  91.2 1.1 paired.8
  92.3 5.0 %collective-permute-start.17 = (f32[2,96,512]{2,1,0:T(8,128)S(1)}, f32[2,96,512]{2,1,0:T(8,128)S(1)}, u32[]{:S(2)}, u32[]{:S(2)}) collective-permute-start(f32[2,96,512]{2,1,0:T(8,128)S(1)} %paired.8), channel_id=1, source_target_pairs={{0,32},{1,225},{32,64},{33,1},{64,96},{65,33},{96,128},{97,65},{12... | collective-permute-start | bytes 1179656 | tf_op jit(solution)/shard_map/ppermute | solution.py:43
  97.3 1.0 paired.11
  98.4 2.1 %collective-permute-start.20 = (f32[2,96,512]{2,1,0:T(8,128)S(1)}, f32[2,96,512]{2,1,0:T(8,128)S(1)}, u32[]{:S(2)}, u32[]{:S(2)}) collective-permute-start(f32[2,96,512]{2,1,0:T(8,128)S(1)} %paired.11), channel_id=1, source_target_pairs={{0,32},{1,225},{32,64},{33,1},{64,96},{65,33},{96,128},{97,65},{12... | collective-permute-start | bytes 1179656 | tf_op jit(solution)/shard_map/ppermute | solution.py:43
  100.5 1.6 %collective-permute-done.17.refs_5_ = f32[2,96,512]{2,1,0:T(8,128)S(1)} collective-permute-done((f32[2,96,512]{2,1,0:T(8,128)S(1)}, f32[2,96,512]{2,1,0:T(8,128)S(1)}, u32[]{:S(2)}, u32[]{:S(2)}) %collective-permute-start.17) | collective-permute-done | bytes 393248 | tf_op jit(solution)/shard_map/ppermute | solution.py:43
  102.0 1.0 paired.9
  103.1 5.0 %collective-permute-start.18 = (f32[2,96,512]{2,1,0:T(8,128)S(1)}, f32[2,96,512]{2,1,0:T(8,128)S(1)}, u32[]{:S(2)}, u32[]{:S(2)}) collective-permute-start(f32[2,96,512]{2,1,0:T(8,128)S(1)} %paired.9), channel_id=1, source_target_pairs={{0,32},{1,225},{32,64},{33,1},{64,96},{65,33},{96,128},{97,65},{12... | collective-permute-start | bytes 1179656 | tf_op jit(solution)/shard_map/ppermute | solution.py:43
  108.1 1.0 paired.12
  109.1 3.2 %collective-permute-start.21 = (f32[2,96,512]{2,1,0:T(8,128)S(1)}, f32[2,96,512]{2,1,0:T(8,128)S(1)}, u32[]{:S(2)}, u32[]{:S(2)}) collective-permute-start(f32[2,96,512]{2,1,0:T(8,128)S(1)} %paired.12), channel_id=1, source_target_pairs={{0,32},{1,225},{32,64},{33,1},{64,96},{65,33},{96,128},{97,65},{12... | collective-permute-start | bytes 1179656 | tf_op jit(solution)/shard_map/ppermute | solution.py:43
  112.3 0.5 collective-permute-done.18.refs_5_
  112.8 1.0 paired.10
  113.8 7.2 %collective-permute-start.19 = (f32[2,96,512]{2,1,0:T(8,128)S(1)}, f32[2,96,512]{2,1,0:T(8,128)S(1)}, u32[]{:S(2)}, u32[]{:S(2)}) collective-permute-start(f32[2,96,512]{2,1,0:T(8,128)S(1)} %paired.10), channel_id=1, source_target_pairs={{0,288},{1,481},{32,320},{33,257},{64,352},{65,289},{96,384},{97,3... | collective-permute-start | bytes 1179656 | tf_op jit(solution)/shard_map/ppermute | solution.py:316
  121.1 1.0 paired.13
  122.1 1.9 %collective-permute-start.22 = (f32[2,96,512]{2,1,0:T(8,128)S(1)}, f32[2,96,512]{2,1,0:T(8,128)S(1)}, u32[]{:S(2)}, u32[]{:S(2)}) collective-permute-start(f32[2,96,512]{2,1,0:T(8,128)S(1)} %paired.13), channel_id=1, source_target_pairs={{0,32},{1,225},{32,64},{33,1},{64,96},{65,33},{96,128},{97,65},{12... | collective-permute-start | bytes 1179656 | tf_op jit(solution)/shard_map/ppermute | solution.py:43
  124.0 1.0 taken.5
  125.0 3.4 %collective-permute-start.13 = (f32[96,512]{1,0:T(8,128)S(1)}, f32[96,512]{1,0:T(8,128)S(1)}, u32[]{:S(2)}, u32[]{:S(2)}) collective-permute-start(f32[96,512]{1,0:T(8,128)S(1)} %bitcast.28), channel_id=1, source_target_pairs={{0,256},{256,0},{1,257},{257,1},{2,258},{258,2},{3,259},{259,3},{4... | collective-permute-start | bytes 589832 | tf_op jit(solution)/shard_map/ppermute | solution.py:308
  128.5 3.0 %collective-permute-done.22 = f32[2,96,512]{2,1,0:T(8,128)S(1)} collective-permute-done((f32[2,96,512]{2,1,0:T(8,128)S(1)}, f32[2,96,512]{2,1,0:T(8,128)S(1)}, u32[]{:S(2)}, u32[]{:S(2)}) %collective-permute-start.22) | collective-permute-done | bytes 393248 | tf_op jit(solution)/shard_map/ppermute | solution.py:43
  131.5 5.3 %collective-permute-start.23 = (f32[96,512]{1,0:T(8,128)S(1)}, f32[96,512]{1,0:T(8,128)}, u32[]{:S(2)}, u32[]{:S(2)}) collective-permute-start(f32[96,512]{1,0:T(8,128)S(1)} %fusion), channel_id=1, source_target_pairs={{0,1},{1,0},{2,3},{3,2},{4,5},{5,4},{6,7},{7,6},{8,9},{9,8},{10,11... | collective-permute-start | bytes 589832 | tf_op jit(solution)/shard_map/ppermute | solution.py:39
  136.8 0.1 dynamic_slice.3
  136.9 0.2 select_reduce_fusion
  137.1 1.0 taken.4
  138.1 1.1 multiply_reduce_fusion
  139.2 0.6 broadcast_in_dim.45
  139.9 4.0 %all-to-all-start = ((f32[32,1,96]{2,1,0:T(1,128)}), f32[32,1,96]{2,1,0:T(1,128)S(1)}, u32[]{:S(2)}, u32[]{:S(2)}) async-start(f32[32,1,96]{2,1,0:T(1,128)} %broadcast_in_dim.45), calls=%async_computation | async-start | bytes 32768 | tf_op jit(solution)/shard_map/all_to_all | solution.py:324
  143.9 0.1 iota_compare_fusion.1
  144.0 0.1 le.23
  144.1 7.6 %all-to-all-done = f32[32,1,96]{2,1,0:T(1,128)S(1)} async-done(((f32[32,1,96]{2,1,0:T(1,128)}), f32[32,1,96]{2,1,0:T(1,128)S(1)}, u32[]{:S(2)}, u32[]{:S(2)}) %all-to-all-start) | async-done | bytes 12320 | tf_op jit(solution)/shard_map/all_to_all | solution.py:324
  151.7 0.7 select_convert_fusion
  (25 shorter events, 0.2 us)
Async XLA Ops:
  2.0 9.8 %collective-permute-start = (bf16[32,3072]{1,0:T(8,128)(2,1)S(1)}, bf16[32,3072]{1,0:T(8,128)(2,1)S(1)}, u32[]{:S(2)}, u32[]{:S(2)}) collective-permute-start(bf16[32,3072]{1,0:T(8,128)(2,1)S(1)} %pick.1.refs_0_), channel_id=1, source_target_pairs={{0,1},{1,0},{2,3},{3,2},{4,5},{5,4},{6,7},{7,6},{8,9},{9,8},{10,11... | collective-permute-start | bytes 589832 | tf_op jit(solution)/shard_map/ppermute | solution.py:39
  11.8 48.6 %copy-start.1 = (s32[256]{0:T(256)S(1)}, s32[256]{0:T(256)}, u32[]{:S(2)}) copy-start(s32[256]{0:T(256)} %param.17) | copy-start | bytes 3076
  11.8 10.0 %collective-permute-start.1 = (bf16[64,3072]{1,0:T(8,128)(2,1)S(1)}, bf16[64,3072]{1,0:T(8,128)(2,1)S(1)}, u32[]{:S(2)}, u32[]{:S(2)}) collective-permute-start(bf16[64,3072]{1,0:T(8,128)(2,1)S(1)} %joined.4.refs_0_), channel_id=1, source_target_pairs={{0,2},{1,15},{2,4},{3,1},{4,6},{5,3},{6,8},{7,5},{8,10},{9,7},{10,... | collective-permute-start | bytes 1179656 | tf_op jit(solution)/shard_map/ppermute | solution.py:43
  17.2 13.3 %collective-permute-start.5 = (bf16[64,3072]{1,0:T(8,128)(2,1)S(1)}, bf16[64,3072]{1,0:T(8,128)(2,1)S(1)}, u32[]{:S(2)}, u32[]{:S(2)}) collective-permute-start(bf16[64,3072]{1,0:T(8,128)(2,1)S(1)} %joined.4.refs_0_), channel_id=1, source_target_pairs={{0,18},{1,31},{2,20},{3,17},{4,22},{5,19},{6,24},{7,21},{8,26},{9,... | collective-permute-start | bytes 1179656 | tf_op jit(solution)/shard_map/ppermute | solution.py:249
  21.9 15.4 %collective-permute-start.2 = (bf16[64,3072]{1,0:T(8,128)(2,1)S(1)}, bf16[64,3072]{1,0:T(8,128)(2,1)S(1)}, u32[]{:S(2)}, u32[]{:S(2)}) collective-permute-start(bf16[64,3072]{1,0:T(8,128)(2,1)S(1)} %collective-permute-done.1.refs_0_), channel_id=1, source_target_pairs={{0,2},{1,15},{2,4},{3,1},{4,6},{5,3},{6,8},{7,5},{8,10},{9,7},{10,... | collective-permute-start | bytes 1179656 | tf_op jit(solution)/shard_map/ppermute | solution.py:43
  30.5 9.3 %collective-permute-start.6 = (bf16[64,3072]{1,0:T(8,128)(2,1)S(1)}, bf16[64,3072]{1,0:T(8,128)(2,1)S(1)}, u32[]{:S(2)}, u32[]{:S(2)}) collective-permute-start(bf16[64,3072]{1,0:T(8,128)(2,1)S(1)} %collective-permute-done.5.refs_1_), channel_id=1, source_target_pairs={{0,2},{1,15},{2,4},{3,1},{4,6},{5,3},{6,8},{7,5},{8,10},{9,7},{10,... | collective-permute-start | bytes 1179656 | tf_op jit(solution)/shard_map/ppermute | solution.py:43
  35.0 9.7 %collective-permute-start.10 = (bf16[32,3072]{1,0:T(8,128)(2,1)S(1)}, bf16[32,3072]{1,0:T(8,128)(2,1)S(1)}, u32[]{:S(2)}, u32[]{:S(2)}) collective-permute-start(bf16[32,3072]{1,0:T(8,128)(2,1)S(1)} %pick.1.refs_0_), channel_id=1, source_target_pairs={{0,16},{16,0},{1,17},{17,1},{2,18},{18,2},{3,19},{19,3},{4,20},{20... | collective-permute-start | bytes 589832 | tf_op jit(solution)/shard_map/ppermute | solution.py:250
  37.2 12.0 %collective-permute-start.3 = (bf16[64,3072]{1,0:T(8,128)(2,1)S(1)}, bf16[64,3072]{1,0:T(8,128)(2,1)S(1)}, u32[]{:S(2)}, u32[]{:S(2)}) collective-permute-start(bf16[64,3072]{1,0:T(8,128)(2,1)S(1)} %collective-permute-done.2.refs_0_), channel_id=1, source_target_pairs={{0,2},{1,15},{2,4},{3,1},{4,6},{5,3},{6,8},{7,5},{8,10},{9,7},{10,... | collective-permute-start | bytes 1179656 | tf_op jit(solution)/shard_map/ppermute | solution.py:43
  39.7 10.5 %collective-permute-start.7 = (bf16[64,3072]{1,0:T(8,128)(2,1)S(1)}, bf16[64,3072]{1,0:T(8,128)(2,1)S(1)}, u32[]{:S(2)}, u32[]{:S(2)}) collective-permute-start(bf16[64,3072]{1,0:T(8,128)(2,1)S(1)} %collective-permute-done.6.refs_1_), channel_id=1, source_target_pairs={{0,2},{1,15},{2,4},{3,1},{4,6},{5,3},{6,8},{7,5},{8,10},{9,7},{10,... | collective-permute-start | bytes 1179656 | tf_op jit(solution)/shard_map/ppermute | solution.py:43
  44.8 18.3 %collective-permute-start.11 = (bf16[160,3072]{1,0:T(8,128)(2,1)S(1)}, bf16[160,3072]{1,0:T(8,128)(2,1)S(1)}, u32[]{:S(2)}, u32[]{:S(2)}) collective-permute-start(bf16[160,3072]{1,0:T(8,128)(2,1)S(1)} %joined.6.refs_4_), channel_id=1, source_target_pairs={{0,1},{1,0},{2,3},{3,2},{4,5},{5,4},{6,7},{7,6},{8,9},{9,8},{10,11... | collective-permute-start | bytes 2949128 | tf_op jit(solution)/shard_map/ppermute | solution.py:39
  46.8 16.3 %collective-permute-start.12 = (bf16[128,3072]{1,0:T(8,128)(2,1)S(1)}, bf16[128,3072]{1,0:T(8,128)(2,1)S(1)}, u32[]{:S(2)}, u32[]{:S(2)}) collective-permute-start(bf16[128,3072]{1,0:T(8,128)(2,1)S(1)} %joined.7.refs_2_), channel_id=1, source_target_pairs={{0,1},{1,0},{2,3},{3,2},{4,5},{5,4},{6,7},{7,6},{8,9},{9,8},{10,11... | collective-permute-start | bytes 2359304 | tf_op jit(solution)/shard_map/ppermute | solution.py:39
  50.3 14.8 %collective-permute-start.9 = (bf16[128,3072]{1,0:T(8,128)(2,1)S(1)}, bf16[128,3072]{1,0:T(8,128)(2,1)S(1)}, u32[]{:S(2)}, u32[]{:S(2)}) collective-permute-start(bf16[128,3072]{1,0:T(8,128)(2,1)S(1)} %joined.5.refs_0_), channel_id=1, source_target_pairs={{0,1},{1,0},{2,3},{3,2},{4,5},{5,4},{6,7},{7,6},{8,9},{9,8},{10,11... | collective-permute-start | bytes 2359304 | tf_op jit(solution)/shard_map/ppermute | solution.py:39
  55.4 10.7 %collective-permute-start.4 = (bf16[64,3072]{1,0:T(8,128)(2,1)S(1)}, bf16[64,3072]{1,0:T(8,128)(2,1)S(1)}, u32[]{:S(2)}, u32[]{:S(2)}) collective-permute-start(bf16[64,3072]{1,0:T(8,128)(2,1)S(1)} %collective-permute-done.3.refs_0_), channel_id=1, source_target_pairs={{0,2},{1,15},{2,4},{3,1},{4,6},{5,3},{6,8},{7,5},{8,10},{9,7},{10,... | collective-permute-start | bytes 1179656 | tf_op jit(solution)/shard_map/ppermute | solution.py:43
  57.8 10.6 %collective-permute-start.8 = (bf16[64,3072]{1,0:T(8,128)(2,1)S(1)}, bf16[64,3072]{1,0:T(8,128)(2,1)S(1)}, u32[]{:S(2)}, u32[]{:S(2)}) collective-permute-start(bf16[64,3072]{1,0:T(8,128)(2,1)S(1)} %collective-permute-done.7.refs_1_), channel_id=1, source_target_pairs={{0,2},{1,15},{2,4},{3,1},{4,6},{5,3},{6,8},{7,5},{8,10},{9,7},{10,... | collective-permute-start | bytes 1179656 | tf_op jit(solution)/shard_map/ppermute | solution.py:43
  72.1 19.1 %collective-permute-start.14 = (f32[6,96,512]{2,1,0:T(8,128)S(1)}, f32[6,96,512]{2,1,0:T(8,128)S(1)}, u32[]{:S(2)}, u32[]{:S(2)}) collective-permute-start(f32[6,96,512]{2,1,0:T(8,128)S(1)} %taken.6), channel_id=1, source_target_pairs={{0,1},{1,0},{2,3},{3,2},{4,5},{5,4},{6,7},{7,6},{8,9},{9,8},{10,11... | collective-permute-start | bytes 3538952 | tf_op jit(solution)/shard_map/ppermute | solution.py:39
  77.1 3.3 %collective-permute-start.15 = (f32[1,96,512]{2,1,0:T(8,128)S(1)}, f32[1,96,512]{2,1,0:T(8,128)S(1)}, u32[]{:S(2)}, u32[]{:S(2)}) collective-permute-start(f32[1,96,512]{2,1,0:T(8,128)S(1)} %taken.7), channel_id=1, source_target_pairs={{0,1},{1,0},{2,3},{3,2},{4,5},{5,4},{6,7},{7,6},{8,9},{9,8},{10,11... | collective-permute-start | bytes 589832 | tf_op jit(solution)/shard_map/ppermute | solution.py:39
  81.4 9.8 %collective-permute-start.16 = (f32[2,96,512]{2,1,0:T(8,128)S(1)}, f32[2,96,512]{2,1,0:T(8,128)S(1)}, u32[]{:S(2)}, u32[]{:S(2)}) collective-permute-start(f32[2,96,512]{2,1,0:T(8,128)S(1)} %paired.7), channel_id=1, source_target_pairs={{0,32},{1,225},{32,64},{33,1},{64,96},{65,33},{96,128},{97,65},{12... | collective-permute-start | bytes 1179656 | tf_op jit(solution)/shard_map/ppermute | solution.py:43
  92.3 9.7 %collective-permute-start.17 = (f32[2,96,512]{2,1,0:T(8,128)S(1)}, f32[2,96,512]{2,1,0:T(8,128)S(1)}, u32[]{:S(2)}, u32[]{:S(2)}) collective-permute-start(f32[2,96,512]{2,1,0:T(8,128)S(1)} %paired.8), channel_id=1, source_target_pairs={{0,32},{1,225},{32,64},{33,1},{64,96},{65,33},{96,128},{97,65},{12... | collective-permute-start | bytes 1179656 | tf_op jit(solution)/shard_map/ppermute | solution.py:43
  98.4 9.7 %collective-permute-start.20 = (f32[2,96,512]{2,1,0:T(8,128)S(1)}, f32[2,96,512]{2,1,0:T(8,128)S(1)}, u32[]{:S(2)}, u32[]{:S(2)}) collective-permute-start(f32[2,96,512]{2,1,0:T(8,128)S(1)} %paired.11), channel_id=1, source_target_pairs={{0,32},{1,225},{32,64},{33,1},{64,96},{65,33},{96,128},{97,65},{12... | collective-permute-start | bytes 1179656 | tf_op jit(solution)/shard_map/ppermute | solution.py:43
  103.1 9.7 %collective-permute-start.18 = (f32[2,96,512]{2,1,0:T(8,128)S(1)}, f32[2,96,512]{2,1,0:T(8,128)S(1)}, u32[]{:S(2)}, u32[]{:S(2)}) collective-permute-start(f32[2,96,512]{2,1,0:T(8,128)S(1)} %paired.9), channel_id=1, source_target_pairs={{0,32},{1,225},{32,64},{33,1},{64,96},{65,33},{96,128},{97,65},{12... | collective-permute-start | bytes 1179656 | tf_op jit(solution)/shard_map/ppermute | solution.py:43
  109.1 11.9 %collective-permute-start.21 = (f32[2,96,512]{2,1,0:T(8,128)S(1)}, f32[2,96,512]{2,1,0:T(8,128)S(1)}, u32[]{:S(2)}, u32[]{:S(2)}) collective-permute-start(f32[2,96,512]{2,1,0:T(8,128)S(1)} %paired.12), channel_id=1, source_target_pairs={{0,32},{1,225},{32,64},{33,1},{64,96},{65,33},{96,128},{97,65},{12... | collective-permute-start | bytes 1179656 | tf_op jit(solution)/shard_map/ppermute | solution.py:43
  113.8 14.6 %collective-permute-start.19 = (f32[2,96,512]{2,1,0:T(8,128)S(1)}, f32[2,96,512]{2,1,0:T(8,128)S(1)}, u32[]{:S(2)}, u32[]{:S(2)}) collective-permute-start(f32[2,96,512]{2,1,0:T(8,128)S(1)} %paired.10), channel_id=1, source_target_pairs={{0,288},{1,481},{32,320},{33,257},{64,352},{65,289},{96,384},{97,3... | collective-permute-start | bytes 1179656 | tf_op jit(solution)/shard_map/ppermute | solution.py:316
  122.1 14.8 %copy-start = (s32[256]{0:T(256)S(1)}, s32[256]{0:T(256)}, u32[]{:S(2)}) copy-start(s32[256]{0:T(256)} %accepted.1) | copy-start | bytes 3076
  122.1 9.3 %collective-permute-start.22 = (f32[2,96,512]{2,1,0:T(8,128)S(1)}, f32[2,96,512]{2,1,0:T(8,128)S(1)}, u32[]{:S(2)}, u32[]{:S(2)}) collective-permute-start(f32[2,96,512]{2,1,0:T(8,128)S(1)} %paired.13), channel_id=1, source_target_pairs={{0,32},{1,225},{32,64},{33,1},{64,96},{65,33},{96,128},{97,65},{12... | collective-permute-start | bytes 1179656 | tf_op jit(solution)/shard_map/ppermute | solution.py:43
  125.0 26.7 %copy-start.2 = (f32[512]{0:T(512)S(1)}, f32[512]{0:T(512)}, u32[]{:S(2)}) copy-start(f32[512]{0:T(512)} %param.15) | copy-start | bytes 6148
  125.0 13.1 %collective-permute-start.13 = (f32[96,512]{1,0:T(8,128)S(1)}, f32[96,512]{1,0:T(8,128)S(1)}, u32[]{:S(2)}, u32[]{:S(2)}) collective-permute-start(f32[96,512]{1,0:T(8,128)S(1)} %bitcast.28), channel_id=1, source_target_pairs={{0,256},{256,0},{1,257},{257,1},{2,258},{258,2},{3,259},{259,3},{4... | collective-permute-start | bytes 589832 | tf_op jit(solution)/shard_map/ppermute | solution.py:308
  131.5 6.6 %collective-permute-start.23 = (f32[96,512]{1,0:T(8,128)S(1)}, f32[96,512]{1,0:T(8,128)}, u32[]{:S(2)}, u32[]{:S(2)}) collective-permute-start(f32[96,512]{1,0:T(8,128)S(1)} %fusion), channel_id=1, source_target_pairs={{0,1},{1,0},{2,3},{3,2},{4,5},{5,4},{6,7},{7,6},{8,9},{9,8},{10,11... | collective-permute-start | bytes 589832 | tf_op jit(solution)/shard_map/ppermute | solution.py:39
  139.9 11.8 %all-to-all-start = ((f32[32,1,96]{2,1,0:T(1,128)}), f32[32,1,96]{2,1,0:T(1,128)S(1)}, u32[]{:S(2)}, u32[]{:S(2)}) async-start(f32[32,1,96]{2,1,0:T(1,128)} %broadcast_in_dim.45), calls=%async_computation | async-start | bytes 32768 | tf_op jit(solution)/shard_map/all_to_all | solution.py:324

commit v3 on v2

--- a/solution.py
+++ b/solution.py
@@ -299,18 +299,25 @@
 
     table = (me, first, turn, partial_value)
     far = taken(table, (1,))
-    behind = taken(table, tuple(range(2, 8)))
+    soon = taken(table, (2, 3))
+    behind = taken(table, tuple(range(4, 8)))
     beyond = taken(table, (8,))[0]
     own = taken(table, (9,))[0]
     far = paired(table, 0, other_core(far), 0)
     far = onward(far, "y")
+    soon = other_core(soon)
     behind = other_core(behind)
     across = lax.ppermute(beyond, "xh", SWAP)
     came = [far, far]
     for step, k in enumerate((3, 2, 1)):
         for v in range(2):
             total = paired(
-                table, 8 + 2 * k + v, behind, 2 * step + v, came[v], step == 0
+                table,
+                8 + 2 * k + v,
+                behind if step else soon,
+                2 * max(step - 1, 0) + v,
+                came[v],
+                step == 0,
             )
             if k == 1 and v == 0:
                 came[v] = lax.ppermute(total, (*TP, "c"), diagonal(ny))

time: 153 us -> 153 us (level)
  waiting for transfers between devices: 28.9 us -> 25.6 us
  starting transfers between devices: 98.5 us -> 101 us
    ppermute x7 -> x8, starting transfers between devices: 29.4 us -> 31.7 us  [other_core(): return lax.ppermute(x, 'c', SWAP)]
    ppermute x13, waiting for transfers between devices: 15.2 us -> 13.3 us  [onward(): return lax.ppermute(x, (axis, 'c'), both_ways(lax.axis_size(axis)))]
    pallas_call x4 -> x5, Pallas kernels: 6.02 us -> 6.58 us  [taken(): pl.pallas_call(kernel, out_shape=jax.ShapeDtypeStruct((len(blocks), first...]
  transfers between devices with their start and end apart: 25 -> 26, of which waited for: 12 -> 11; matrix products, arithmetic and copies ran while one was open for 0% -> 0% of each run, Pallas kernels for 10% -> 12%
where the time goes in v3:
time: 153 us; the launch traced here: 152 us
  starting transfers between devices  101 us (66%)
  waiting for transfers between devices  25.6 us (17%)
  Pallas kernels  22 us (14%)
  other arithmetic  2.23 us (1%)
    ppermute x13, starting transfers between devices, onward(): return lax.ppermute(x, (axis, 'c'), both_ways(lax.axis_size(axis)))  49.1 us
    ppermute x8, starting transfers between devices, other_core(): return lax.ppermute(x, 'c', SWAP)  31.7 us
    ppermute x13, waiting for transfers between devices, onward(): return lax.ppermute(x, (axis, 'c'), both_ways(lax.axis_size(axis)))  13.3 us
    all_to_all x1, waiting for transfers between devices, step_on_device(): lax.all_to_all(jnp.broadcast_to(squares[None], (4 * nz, size)), GRP, 0, 0...  7.61 us
    pallas_call x7, Pallas kernels, paired(): pl.pallas_call(kernel, out_shape=jax.ShapeDtypeStruct((2, *theirs.shape[1...  7.24 us
    ppermute x1, starting transfers between devices, step_on_device(): came[v] = lax.ppermute(total, (*TP, 'c'), diagonal(ny))  7.21 us
    pallas_call x5, Pallas kernels, taken(): pl.pallas_call(kernel, out_shape=jax.ShapeDtypeStruct((len(blocks), first...  6.58 us
    pallas_call x4, Pallas kernels, product(): pl.pallas_call(kernel, out_shape=shapes, in_specs=[VMEM] * len(arrays) +...  6.1 us
  transfers between devices with their start and end apart: 26, of which 11 were waited for; matrix products, arithmetic and copies ran while one was open for 0% of the time, Pallas kernels for 12%

profile of v3, /device:TPU:1, one launch (start us, length us, event | category | flops | bytes accessed | tf_op | source)
XLA Modules:
  0.0 152.0 jit_solution(8136649635313271372)
XLA Ops:
  0.0 0.1 stack.23.me.refs_0_
  0.1 1.9 %pick.1.refs_0_ = bf16[32,3072]{1,0:T(8,128)(2,1)S(1)} custom-call(s32[5]{0:T(128)S(1)} %stack.23.me.refs_0_, s32[256]{0:T(256)} %accepted.1, bf16[48,1024]{1,0:T(8,128)(2,1)} %low.1, bf16[48,1024]{1,0:T(8,128)(2,1)} %mid.1, bf16[48,1024]{1,0:T(8,128)(2,1)} %high.1), custom_call_target="tpu_custom_call" | custom-call | tf_op jit(solution)/shard_map/pick/pallas_call | solution.py:165
  2.0 8.7 %collective-permute-start = (bf16[32,3072]{1,0:T(8,128)(2,1)S(1)}, bf16[32,3072]{1,0:T(8,128)(2,1)S(1)}, u32[]{:S(2)}, u32[]{:S(2)}) collective-permute-start(bf16[32,3072]{1,0:T(8,128)(2,1)S(1)} %pick.1.refs_0_), channel_id=1, source_target_pairs={{0,1},{1,0},{2,3},{3,2},{4,5},{5,4},{6,7},{7,6},{8,9},{9,8},{10,11... | collective-permute-start | bytes 589832 | tf_op jit(solution)/shard_map/ppermute | solution.py:39
  10.7 1.0 collective-permute-done.refs_1_
  11.8 5.3 %collective-permute-start.1 = (bf16[64,3072]{1,0:T(8,128)(2,1)S(1)}, bf16[64,3072]{1,0:T(8,128)(2,1)S(1)}, u32[]{:S(2)}, u32[]{:S(2)}) collective-permute-start(bf16[64,3072]{1,0:T(8,128)(2,1)S(1)} %joined.4.refs_0_), channel_id=1, source_target_pairs={{0,2},{1,15},{2,4},{3,1},{4,6},{5,3},{6,8},{7,5},{8,10},{9,7},{10,... | collective-permute-start | bytes 1179656 | tf_op jit(solution)/shard_map/ppermute | solution.py:43
  17.2 3.1 %collective-permute-start.5 = (bf16[64,3072]{1,0:T(8,128)(2,1)S(1)}, bf16[64,3072]{1,0:T(8,128)(2,1)S(1)}, u32[]{:S(2)}, u32[]{:S(2)}) collective-permute-start(bf16[64,3072]{1,0:T(8,128)(2,1)S(1)} %joined.4.refs_0_), channel_id=1, source_target_pairs={{0,18},{1,31},{2,20},{3,17},{4,22},{5,19},{6,24},{7,21},{8,26},{9,... | collective-permute-start | bytes 1179656 | tf_op jit(solution)/shard_map/ppermute | solution.py:249
  20.3 1.6 %collective-permute-done.1.refs_0_ = bf16[64,3072]{1,0:T(8,128)(2,1)S(1)} collective-permute-done((bf16[64,3072]{1,0:T(8,128)(2,1)S(1)}, bf16[64,3072]{1,0:T(8,128)(2,1)S(1)}, u32[]{:S(2)}, u32[]{:S(2)}) %collective-permute-start.1) | collective-permute-done | bytes 393248 | tf_op jit(solution)/shard_map/ppermute | solution.py:43
  21.9 5.0 %collective-permute-start.2 = (bf16[64,3072]{1,0:T(8,128)(2,1)S(1)}, bf16[64,3072]{1,0:T(8,128)(2,1)S(1)}, u32[]{:S(2)}, u32[]{:S(2)}) collective-permute-start(bf16[64,3072]{1,0:T(8,128)(2,1)S(1)} %collective-permute-done.1.refs_0_), channel_id=1, source_target_pairs={{0,2},{1,15},{2,4},{3,1},{4,6},{5,3},{6,8},{7,5},{8,10},{9,7},{10,... | collective-permute-start | bytes 1179656 | tf_op jit(solution)/shard_map/ppermute | solution.py:43
  26.9 3.6 %collective-permute-done.5.refs_1_ = bf16[64,3072]{1,0:T(8,128)(2,1)S(1)} collective-permute-done((bf16[64,3072]{1,0:T(8,128)(2,1)S(1)}, bf16[64,3072]{1,0:T(8,128)(2,1)S(1)}, u32[]{:S(2)}, u32[]{:S(2)}) %collective-permute-start.5) | collective-permute-done | bytes 393248 | tf_op jit(solution)/shard_map/ppermute | solution.py:249
  30.4 4.6 %collective-permute-start.6 = (bf16[64,3072]{1,0:T(8,128)(2,1)S(1)}, bf16[64,3072]{1,0:T(8,128)(2,1)S(1)}, u32[]{:S(2)}, u32[]{:S(2)}) collective-permute-start(bf16[64,3072]{1,0:T(8,128)(2,1)S(1)} %collective-permute-done.5.refs_1_), channel_id=1, source_target_pairs={{0,2},{1,15},{2,4},{3,1},{4,6},{5,3},{6,8},{7,5},{8,10},{9,7},{10,... | collective-permute-start | bytes 1179656 | tf_op jit(solution)/shard_map/ppermute | solution.py:43
  35.0 2.2 %collective-permute-start.10 = (bf16[32,3072]{1,0:T(8,128)(2,1)S(1)}, bf16[32,3072]{1,0:T(8,128)(2,1)S(1)}, u32[]{:S(2)}, u32[]{:S(2)}) collective-permute-start(bf16[32,3072]{1,0:T(8,128)(2,1)S(1)} %pick.1.refs_0_), channel_id=1, source_target_pairs={{0,16},{16,0},{1,17},{17,1},{2,18},{18,2},{3,19},{19,3},{4,20},{20... | collective-permute-start | bytes 589832 | tf_op jit(solution)/shard_map/ppermute | solution.py:250
  37.2 1.9 %collective-permute-start.3 = (bf16[64,3072]{1,0:T(8,128)(2,1)S(1)}, bf16[64,3072]{1,0:T(8,128)(2,1)S(1)}, u32[]{:S(2)}, u32[]{:S(2)}) collective-permute-start(bf16[64,3072]{1,0:T(8,128)(2,1)S(1)} %collective-permute-done.2.refs_0_), channel_id=1, source_target_pairs={{0,2},{1,15},{2,4},{3,1},{4,6},{5,3},{6,8},{7,5},{8,10},{9,7},{10,... | collective-permute-start | bytes 1179656 | tf_op jit(solution)/shard_map/ppermute | solution.py:43
  39.1 0.6 collective-permute-done.6.refs_1_
  39.7 5.0 %collective-permute-start.7 = (bf16[64,3072]{1,0:T(8,128)(2,1)S(1)}, bf16[64,3072]{1,0:T(8,128)(2,1)S(1)}, u32[]{:S(2)}, u32[]{:S(2)}) collective-permute-start(bf16[64,3072]{1,0:T(8,128)(2,1)S(1)} %collective-permute-done.6.refs_1_), channel_id=1, source_target_pairs={{0,2},{1,15},{2,4},{3,1},{4,6},{5,3},{6,8},{7,5},{8,10},{9,7},{10,... | collective-permute-start | bytes 1179656 | tf_op jit(solution)/shard_map/ppermute | solution.py:43
  44.8 0.1 joined.6.refs_4_
  44.8 1.9 %collective-permute-start.11 = (bf16[160,3072]{1,0:T(8,128)(2,1)S(1)}, bf16[160,3072]{1,0:T(8,128)(2,1)S(1)}, u32[]{:S(2)}, u32[]{:S(2)}) collective-permute-start(bf16[160,3072]{1,0:T(8,128)(2,1)S(1)} %joined.6.refs_4_), channel_id=1, source_target_pairs={{0,1},{1,0},{2,3},{3,2},{4,5},{5,4},{6,7},{7,6},{8,9},{9,8},{10,11... | collective-permute-start | bytes 2949128 | tf_op jit(solution)/shard_map/ppermute | solution.py:39
  46.8 2.4 %collective-permute-start.12 = (bf16[128,3072]{1,0:T(8,128)(2,1)S(1)}, bf16[128,3072]{1,0:T(8,128)(2,1)S(1)}, u32[]{:S(2)}, u32[]{:S(2)}) collective-permute-start(bf16[128,3072]{1,0:T(8,128)(2,1)S(1)} %joined.7.refs_2_), channel_id=1, source_target_pairs={{0,1},{1,0},{2,3},{3,2},{4,5},{5,4},{6,7},{7,6},{8,9},{9,8},{10,11... | collective-permute-start | bytes 2359304 | tf_op jit(solution)/shard_map/ppermute | solution.py:39
  49.3 1.0 collective-permute-done.7.refs_1_
  50.3 5.1 %collective-permute-start.9 = (bf16[128,3072]{1,0:T(8,128)(2,1)S(1)}, bf16[128,3072]{1,0:T(8,128)(2,1)S(1)}, u32[]{:S(2)}, u32[]{:S(2)}) collective-permute-start(bf16[128,3072]{1,0:T(8,128)(2,1)S(1)} %joined.5.refs_0_), channel_id=1, source_target_pairs={{0,1},{1,0},{2,3},{3,2},{4,5},{5,4},{6,7},{7,6},{8,9},{9,8},{10,11... | collective-permute-start | bytes 2359304 | tf_op jit(solution)/shard_map/ppermute | solution.py:39
  55.4 2.4 %collective-permute-start.4 = (bf16[64,3072]{1,0:T(8,128)(2,1)S(1)}, bf16[64,3072]{1,0:T(8,128)(2,1)S(1)}, u32[]{:S(2)}, u32[]{:S(2)}) collective-permute-start(bf16[64,3072]{1,0:T(8,128)(2,1)S(1)} %collective-permute-done.3.refs_0_), channel_id=1, source_target_pairs={{0,2},{1,15},{2,4},{3,1},{4,6},{5,3},{6,8},{7,5},{8,10},{9,7},{10,... | collective-permute-start | bytes 1179656 | tf_op jit(solution)/shard_map/ppermute | solution.py:43
  57.8 2.6 %collective-permute-start.8 = (bf16[64,3072]{1,0:T(8,128)(2,1)S(1)}, bf16[64,3072]{1,0:T(8,128)(2,1)S(1)}, u32[]{:S(2)}, u32[]{:S(2)}) collective-permute-start(bf16[64,3072]{1,0:T(8,128)(2,1)S(1)} %collective-permute-done.7.refs_1_), channel_id=1, source_target_pairs={{0,2},{1,15},{2,4},{3,1},{4,6},{5,3},{6,8},{7,5},{8,10},{9,7},{10,... | collective-permute-start | bytes 1179656 | tf_op jit(solution)/shard_map/ppermute | solution.py:43
  60.5 0.1 fusion.9.first.refs_1_
  60.5 2.5 %product.4 = (f32[1024,512]{1,0:T(8,128)S(1)}, bf16[3072,512]{1,0:T(8,128)(2,1)S(1)}) custom-call(bf16[64,3072]{1,0:T(8,128)(2,1)S(1)} %joined.4.refs_0_, bf16[1024,512]{1,0:T(8,128)(2,1)} %refs_1_.1, bf16[1024,512]{1,0:T(8,128)(2,1)} %refs_2_.1, bf16[1024,512]{1,0:T(8,128)(2,1)} %refs_3_.1), custom_call_target="tpu_custom_call" | custom-call | tf_op jit(solution)/shard_map/product/pallas_call | solution.py:222
  63.1 2.0 %product.5 = (f32[1024,512]{1,0:T(8,128)S(1)}, bf16[3072,512]{1,0:T(8,128)(2,1)S(1)}) custom-call(bf16[32,3072]{1,0:T(8,128)(2,1)S(1)} %collective-permute-done.10.refs_2_.refs_0_, bf16[160,3072]{1,0:T(8,128)(2,1)S(1)} %collective-permute-done.11.refs_1_, bf16[128,3072]{1,0:T(8,128)(2,1)S(1)} %joined.7.refs_2_, ...), custom_call_target="tpu_custom_call", output_to_operand_aliasing={{0}: (6, {}), {1}: (5, {})} | custom-call | tf_op jit(solution)/shard_map/product/pallas_call | solution.py:222
  65.1 1.0 product.6
  66.1 2.3 %collective-permute-done.8.refs_1_ = bf16[64,3072]{1,0:T(8,128)(2,1)S(1)} collective-permute-done((bf16[64,3072]{1,0:T(8,128)(2,1)S(1)}, bf16[64,3072]{1,0:T(8,128)(2,1)S(1)}, u32[]{:S(2)}, u32[]{:S(2)}) %collective-permute-start.8) | collective-permute-done | bytes 393248 | tf_op jit(solution)/shard_map/ppermute | solution.py:43
  68.4 0.6 product.7
  69.0 1.0 taken.9
  70.0 4.0 %collective-permute-start.16 = (f32[1,96,512]{2,1,0:T(8,128)S(1)}, f32[1,96,512]{2,1,0:T(8,128)S(1)}, u32[]{:S(2)}, u32[]{:S(2)}) collective-permute-start(f32[1,96,512]{2,1,0:T(8,128)S(1)} %taken.9), channel_id=1, source_target_pairs={{0,1},{1,0},{2,3},{3,2},{4,5},{5,4},{6,7},{7,6},{8,9},{9,8},{10,11... | collective-permute-start | bytes 589832 | tf_op jit(solution)/shard_map/ppermute | solution.py:39
  74.0 1.4 taken.8
  75.4 2.2 %taken.7 = f32[4,96,512]{2,1,0:T(8,128)S(1)} custom-call(s32[5]{0:T(128)S(1)} %stack.23.me.refs_0_, s32[256]{0:T(256)S(1)} %fusion.9.first.refs_1_, s32[256]{0:T(256)S(1)} %get-tuple-element.21.turn.refs_2_, f32[1024,512]{1,0:T(8,128)S(1)} %get-tuple-element.18.values.refs_3_), custom_call_target="tpu_custom_call" | custom-call | tf_op jit(solution)/shard_map/taken/pallas_call | solution.py:98
  77.7 1.9 %collective-permute-start.15 = (f32[2,96,512]{2,1,0:T(8,128)S(1)}, f32[2,96,512]{2,1,0:T(8,128)S(1)}, u32[]{:S(2)}, u32[]{:S(2)}) collective-permute-start(f32[2,96,512]{2,1,0:T(8,128)S(1)} %taken.8), channel_id=1, source_target_pairs={{0,1},{1,0},{2,3},{3,2},{4,5},{5,4},{6,7},{7,6},{8,9},{9,8},{10,11... | collective-permute-start | bytes 1179656 | tf_op jit(solution)/shard_map/ppermute | solution.py:39
  79.6 1.0 paired.7
  80.6 5.1 %collective-permute-start.17 = (f32[2,96,512]{2,1,0:T(8,128)S(1)}, f32[2,96,512]{2,1,0:T(8,128)S(1)}, u32[]{:S(2)}, u32[]{:S(2)}) collective-permute-start(f32[2,96,512]{2,1,0:T(8,128)S(1)} %paired.7), channel_id=1, source_target_pairs={{0,32},{1,225},{32,64},{33,1},{64,96},{65,33},{96,128},{97,65},{12... | collective-permute-start | bytes 1179656 | tf_op jit(solution)/shard_map/ppermute | solution.py:43
  85.7 1.9 %collective-permute-start.14 = (f32[4,96,512]{2,1,0:T(8,128)S(1)}, f32[4,96,512]{2,1,0:T(8,128)S(1)}, u32[]{:S(2)}, u32[]{:S(2)}) collective-permute-start(f32[4,96,512]{2,1,0:T(8,128)S(1)} %taken.7), channel_id=1, source_target_pairs={{0,1},{1,0},{2,3},{3,2},{4,5},{5,4},{6,7},{7,6},{8,9},{9,8},{10,11... | collective-permute-start | bytes 2359304 | tf_op jit(solution)/shard_map/ppermute | solution.py:39
  87.6 2.8 %collective-permute-done.17.refs_5_ = f32[2,96,512]{2,1,0:T(8,128)S(1)} collective-permute-done((f32[2,96,512]{2,1,0:T(8,128)S(1)}, f32[2,96,512]{2,1,0:T(8,128)S(1)}, u32[]{:S(2)}, u32[]{:S(2)}) %collective-permute-start.17) | collective-permute-done | bytes 393248 | tf_op jit(solution)/shard_map/ppermute | solution.py:43
  90.4 1.1 paired.8
  91.5 5.0 %collective-permute-start.18 = (f32[2,96,512]{2,1,0:T(8,128)S(1)}, f32[2,96,512]{2,1,0:T(8,128)S(1)}, u32[]{:S(2)}, u32[]{:S(2)}) collective-permute-start(f32[2,96,512]{2,1,0:T(8,128)S(1)} %paired.8), channel_id=1, source_target_pairs={{0,32},{1,225},{32,64},{33,1},{64,96},{65,33},{96,128},{97,65},{12... | collective-permute-start | bytes 1179656 | tf_op jit(solution)/shard_map/ppermute | solution.py:43
  96.5 1.1 paired.11
  97.6 2.1 %collective-permute-start.21 = (f32[2,96,512]{2,1,0:T(8,128)S(1)}, f32[2,96,512]{2,1,0:T(8,128)S(1)}, u32[]{:S(2)}, u32[]{:S(2)}) collective-permute-start(f32[2,96,512]{2,1,0:T(8,128)S(1)} %paired.11), channel_id=1, source_target_pairs={{0,32},{1,225},{32,64},{33,1},{64,96},{65,33},{96,128},{97,65},{12... | collective-permute-start | bytes 1179656 | tf_op jit(solution)/shard_map/ppermute | solution.py:43
  99.6 1.6 %collective-permute-done.18.refs_5_ = f32[2,96,512]{2,1,0:T(8,128)S(1)} collective-permute-done((f32[2,96,512]{2,1,0:T(8,128)S(1)}, f32[2,96,512]{2,1,0:T(8,128)S(1)}, u32[]{:S(2)}, u32[]{:S(2)}) %collective-permute-start.18) | collective-permute-done | bytes 393248 | tf_op jit(solution)/shard_map/ppermute | solution.py:43
  101.2 1.0 paired.9
  102.2 5.0 %collective-permute-start.19 = (f32[2,96,512]{2,1,0:T(8,128)S(1)}, f32[2,96,512]{2,1,0:T(8,128)S(1)}, u32[]{:S(2)}, u32[]{:S(2)}) collective-permute-start(f32[2,96,512]{2,1,0:T(8,128)S(1)} %paired.9), channel_id=1, source_target_pairs={{0,32},{1,225},{32,64},{33,1},{64,96},{65,33},{96,128},{97,65},{12... | collective-permute-start | bytes 1179656 | tf_op jit(solution)/shard_map/ppermute | solution.py:43
  107.3 1.0 paired.12
  108.3 3.2 %collective-permute-start.22 = (f32[2,96,512]{2,1,0:T(8,128)S(1)}, f32[2,96,512]{2,1,0:T(8,128)S(1)}, u32[]{:S(2)}, u32[]{:S(2)}) collective-permute-start(f32[2,96,512]{2,1,0:T(8,128)S(1)} %paired.12), channel_id=1, source_target_pairs={{0,32},{1,225},{32,64},{33,1},{64,96},{65,33},{96,128},{97,65},{12... | collective-permute-start | bytes 1179656 | tf_op jit(solution)/shard_map/ppermute | solution.py:43
  111.5 0.5 collective-permute-done.19.refs_5_
  112.0 1.0 paired.10
  113.0 7.2 %collective-permute-start.20 = (f32[2,96,512]{2,1,0:T(8,128)S(1)}, f32[2,96,512]{2,1,0:T(8,128)S(1)}, u32[]{:S(2)}, u32[]{:S(2)}) collective-permute-start(f32[2,96,512]{2,1,0:T(8,128)S(1)} %paired.10), channel_id=1, source_target_pairs={{0,288},{1,481},{32,320},{33,257},{64,352},{65,289},{96,384},{97,3... | collective-permute-start | bytes 1179656 | tf_op jit(solution)/shard_map/ppermute | solution.py:323
  120.2 1.0 paired.13
  121.3 1.9 %collective-permute-start.23 = (f32[2,96,512]{2,1,0:T(8,128)S(1)}, f32[2,96,512]{2,1,0:T(8,128)S(1)}, u32[]{:S(2)}, u32[]{:S(2)}) collective-permute-start(f32[2,96,512]{2,1,0:T(8,128)S(1)} %paired.13), channel_id=1, source_target_pairs={{0,32},{1,225},{32,64},{33,1},{64,96},{65,33},{96,128},{97,65},{12... | collective-permute-start | bytes 1179656 | tf_op jit(solution)/shard_map/ppermute | solution.py:43
  123.2 1.0 taken.6
  124.2 3.4 %collective-permute-start.13 = (f32[96,512]{1,0:T(8,128)S(1)}, f32[96,512]{1,0:T(8,128)S(1)}, u32[]{:S(2)}, u32[]{:S(2)}) collective-permute-start(f32[96,512]{1,0:T(8,128)S(1)} %bitcast.28), channel_id=1, source_target_pairs={{0,256},{256,0},{1,257},{257,1},{2,258},{258,2},{3,259},{259,3},{4... | collective-permute-start | bytes 589832 | tf_op jit(solution)/shard_map/ppermute | solution.py:310
  127.6 3.0 %collective-permute-done.23 = f32[2,96,512]{2,1,0:T(8,128)S(1)} collective-permute-done((f32[2,96,512]{2,1,0:T(8,128)S(1)}, f32[2,96,512]{2,1,0:T(8,128)S(1)}, u32[]{:S(2)}, u32[]{:S(2)}) %collective-permute-start.23) | collective-permute-done | bytes 393248 | tf_op jit(solution)/shard_map/ppermute | solution.py:43
  130.6 5.7 %collective-permute-start.24 = (f32[96,512]{1,0:T(8,128)S(1)}, f32[96,512]{1,0:T(8,128)}, u32[]{:S(2)}, u32[]{:S(2)}) collective-permute-start(f32[96,512]{1,0:T(8,128)S(1)} %fusion), channel_id=1, source_target_pairs={{0,1},{1,0},{2,3},{3,2},{4,5},{5,4},{6,7},{7,6},{8,9},{9,8},{10,11... | collective-permute-start | bytes 589832 | tf_op jit(solution)/shard_map/ppermute | solution.py:39
  136.4 0.1 dynamic_slice.3
  136.5 0.2 select_reduce_fusion
  136.6 1.0 taken.5
  137.6 1.1 multiply_reduce_fusion
  138.8 0.6 broadcast_in_dim.45
  139.4 4.0 %all-to-all-start = ((f32[32,1,96]{2,1,0:T(1,128)}), f32[32,1,96]{2,1,0:T(1,128)S(1)}, u32[]{:S(2)}, u32[]{:S(2)}) async-start(f32[32,1,96]{2,1,0:T(1,128)} %broadcast_in_dim.45), calls=%async_computation | async-start | bytes 32768 | tf_op jit(solution)/shard_map/all_to_all | solution.py:331
  143.4 0.1 iota_compare_fusion.1
  143.5 0.1 le.23
  143.6 7.6 %all-to-all-done = f32[32,1,96]{2,1,0:T(1,128)S(1)} async-done(((f32[32,1,96]{2,1,0:T(1,128)}), f32[32,1,96]{2,1,0:T(1,128)S(1)}, u32[]{:S(2)}, u32[]{:S(2)}) %all-to-all-start) | async-done | bytes 12320 | tf_op jit(solution)/shard_map/all_to_all | solution.py:331
  151.3 0.7 select_convert_fusion
  (28 shorter events, 0.3 us)
Async XLA Ops:
  0.1 60.4 %copy-start.1 = (s32[256]{0:T(256)S(1)}, s32[256]{0:T(256)}, u32[]{:S(2)}) copy-start(s32[256]{0:T(256)} %param.17) | copy-start | bytes 3076
  2.0 9.8 %collective-permute-start = (bf16[32,3072]{1,0:T(8,128)(2,1)S(1)}, bf16[32,3072]{1,0:T(8,128)(2,1)S(1)}, u32[]{:S(2)}, u32[]{:S(2)}) collective-permute-start(bf16[32,3072]{1,0:T(8,128)(2,1)S(1)} %pick.1.refs_0_), channel_id=1, source_target_pairs={{0,1},{1,0},{2,3},{3,2},{4,5},{5,4},{6,7},{7,6},{8,9},{9,8},{10,11... | collective-permute-start | bytes 589832 | tf_op jit(solution)/shard_map/ppermute | solution.py:39
  11.8 10.0 %collective-permute-start.1 = (bf16[64,3072]{1,0:T(8,128)(2,1)S(1)}, bf16[64,3072]{1,0:T(8,128)(2,1)S(1)}, u32[]{:S(2)}, u32[]{:S(2)}) collective-permute-start(bf16[64,3072]{1,0:T(8,128)(2,1)S(1)} %joined.4.refs_0_), channel_id=1, source_target_pairs={{0,2},{1,15},{2,4},{3,1},{4,6},{5,3},{6,8},{7,5},{8,10},{9,7},{10,... | collective-permute-start | bytes 1179656 | tf_op jit(solution)/shard_map/ppermute | solution.py:43
  17.2 13.3 %collective-permute-start.5 = (bf16[64,3072]{1,0:T(8,128)(2,1)S(1)}, bf16[64,3072]{1,0:T(8,128)(2,1)S(1)}, u32[]{:S(2)}, u32[]{:S(2)}) collective-permute-start(bf16[64,3072]{1,0:T(8,128)(2,1)S(1)} %joined.4.refs_0_), channel_id=1, source_target_pairs={{0,18},{1,31},{2,20},{3,17},{4,22},{5,19},{6,24},{7,21},{8,26},{9,... | collective-permute-start | bytes 1179656 | tf_op jit(solution)/shard_map/ppermute | solution.py:249
  21.9 15.4 %collective-permute-start.2 = (bf16[64,3072]{1,0:T(8,128)(2,1)S(1)}, bf16[64,3072]{1,0:T(8,128)(2,1)S(1)}, u32[]{:S(2)}, u32[]{:S(2)}) collective-permute-start(bf16[64,3072]{1,0:T(8,128)(2,1)S(1)} %collective-permute-done.1.refs_0_), channel_id=1, source_target_pairs={{0,2},{1,15},{2,4},{3,1},{4,6},{5,3},{6,8},{7,5},{8,10},{9,7},{10,... | collective-permute-start | bytes 1179656 | tf_op jit(solution)/shard_map/ppermute | solution.py:43
  30.4 9.3 %collective-permute-start.6 = (bf16[64,3072]{1,0:T(8,128)(2,1)S(1)}, bf16[64,3072]{1,0:T(8,128)(2,1)S(1)}, u32[]{:S(2)}, u32[]{:S(2)}) collective-permute-start(bf16[64,3072]{1,0:T(8,128)(2,1)S(1)} %collective-permute-done.5.refs_1_), channel_id=1, source_target_pairs={{0,2},{1,15},{2,4},{3,1},{4,6},{5,3},{6,8},{7,5},{8,10},{9,7},{10,... | collective-permute-start | bytes 1179656 | tf_op jit(solution)/shard_map/ppermute | solution.py:43
  35.0 9.7 %collective-permute-start.10 = (bf16[32,3072]{1,0:T(8,128)(2,1)S(1)}, bf16[32,3072]{1,0:T(8,128)(2,1)S(1)}, u32[]{:S(2)}, u32[]{:S(2)}) collective-permute-start(bf16[32,3072]{1,0:T(8,128)(2,1)S(1)} %pick.1.refs_0_), channel_id=1, source_target_pairs={{0,16},{16,0},{1,17},{17,1},{2,18},{18,2},{3,19},{19,3},{4,20},{20... | collective-permute-start | bytes 589832 | tf_op jit(solution)/shard_map/ppermute | solution.py:250
  37.2 12.0 %collective-permute-start.3 = (bf16[64,3072]{1,0:T(8,128)(2,1)S(1)}, bf16[64,3072]{1,0:T(8,128)(2,1)S(1)}, u32[]{:S(2)}, u32[]{:S(2)}) collective-permute-start(bf16[64,3072]{1,0:T(8,128)(2,1)S(1)} %collective-permute-done.2.refs_0_), channel_id=1, source_target_pairs={{0,2},{1,15},{2,4},{3,1},{4,6},{5,3},{6,8},{7,5},{8,10},{9,7},{10,... | collective-permute-start | bytes 1179656 | tf_op jit(solution)/shard_map/ppermute | solution.py:43
  39.7 10.5 %collective-permute-start.7 = (bf16[64,3072]{1,0:T(8,128)(2,1)S(1)}, bf16[64,3072]{1,0:T(8,128)(2,1)S(1)}, u32[]{:S(2)}, u32[]{:S(2)}) collective-permute-start(bf16[64,3072]{1,0:T(8,128)(2,1)S(1)} %collective-permute-done.6.refs_1_), channel_id=1, source_target_pairs={{0,2},{1,15},{2,4},{3,1},{4,6},{5,3},{6,8},{7,5},{8,10},{9,7},{10,... | collective-permute-start | bytes 1179656 | tf_op jit(solution)/shard_map/ppermute | solution.py:43
  44.8 18.2 %collective-permute-start.11 = (bf16[160,3072]{1,0:T(8,128)(2,1)S(1)}, bf16[160,3072]{1,0:T(8,128)(2,1)S(1)}, u32[]{:S(2)}, u32[]{:S(2)}) collective-permute-start(bf16[160,3072]{1,0:T(8,128)(2,1)S(1)} %joined.6.refs_4_), channel_id=1, source_target_pairs={{0,1},{1,0},{2,3},{3,2},{4,5},{5,4},{6,7},{7,6},{8,9},{9,8},{10,11... | collective-permute-start | bytes 2949128 | tf_op jit(solution)/shard_map/ppermute | solution.py:39
  46.8 16.2 %collective-permute-start.12 = (bf16[128,3072]{1,0:T(8,128)(2,1)S(1)}, bf16[128,3072]{1,0:T(8,128)(2,1)S(1)}, u32[]{:S(2)}, u32[]{:S(2)}) collective-permute-start(bf16[128,3072]{1,0:T(8,128)(2,1)S(1)} %joined.7.refs_2_), channel_id=1, source_target_pairs={{0,1},{1,0},{2,3},{3,2},{4,5},{5,4},{6,7},{7,6},{8,9},{9,8},{10,11... | collective-permute-start | bytes 2359304 | tf_op jit(solution)/shard_map/ppermute | solution.py:39
  50.3 14.8 %collective-permute-start.9 = (bf16[128,3072]{1,0:T(8,128)(2,1)S(1)}, bf16[128,3072]{1,0:T(8,128)(2,1)S(1)}, u32[]{:S(2)}, u32[]{:S(2)}) collective-permute-start(bf16[128,3072]{1,0:T(8,128)(2,1)S(1)} %joined.5.refs_0_), channel_id=1, source_target_pairs={{0,1},{1,0},{2,3},{3,2},{4,5},{5,4},{6,7},{7,6},{8,9},{9,8},{10,11... | collective-permute-start | bytes 2359304 | tf_op jit(solution)/shard_map/ppermute | solution.py:39
  55.4 10.7 %collective-permute-start.4 = (bf16[64,3072]{1,0:T(8,128)(2,1)S(1)}, bf16[64,3072]{1,0:T(8,128)(2,1)S(1)}, u32[]{:S(2)}, u32[]{:S(2)}) collective-permute-start(bf16[64,3072]{1,0:T(8,128)(2,1)S(1)} %collective-permute-done.3.refs_0_), channel_id=1, source_target_pairs={{0,2},{1,15},{2,4},{3,1},{4,6},{5,3},{6,8},{7,5},{8,10},{9,7},{10,... | collective-permute-start | bytes 1179656 | tf_op jit(solution)/shard_map/ppermute | solution.py:43
  57.8 10.6 %collective-permute-start.8 = (bf16[64,3072]{1,0:T(8,128)(2,1)S(1)}, bf16[64,3072]{1,0:T(8,128)(2,1)S(1)}, u32[]{:S(2)}, u32[]{:S(2)}) collective-permute-start(bf16[64,3072]{1,0:T(8,128)(2,1)S(1)} %collective-permute-done.7.refs_1_), channel_id=1, source_target_pairs={{0,2},{1,15},{2,4},{3,1},{4,6},{5,3},{6,8},{7,5},{8,10},{9,7},{10,... | collective-permute-start | bytes 1179656 | tf_op jit(solution)/shard_map/ppermute | solution.py:43
  70.0 9.6 %collective-permute-start.16 = (f32[1,96,512]{2,1,0:T(8,128)S(1)}, f32[1,96,512]{2,1,0:T(8,128)S(1)}, u32[]{:S(2)}, u32[]{:S(2)}) collective-permute-start(f32[1,96,512]{2,1,0:T(8,128)S(1)} %taken.9), channel_id=1, source_target_pairs={{0,1},{1,0},{2,3},{3,2},{4,5},{5,4},{6,7},{7,6},{8,9},{9,8},{10,11... | collective-permute-start | bytes 589832 | tf_op jit(solution)/shard_map/ppermute | solution.py:39
  77.7 10.0 %collective-permute-start.15 = (f32[2,96,512]{2,1,0:T(8,128)S(1)}, f32[2,96,512]{2,1,0:T(8,128)S(1)}, u32[]{:S(2)}, u32[]{:S(2)}) collective-permute-start(f32[2,96,512]{2,1,0:T(8,128)S(1)} %taken.8), channel_id=1, source_target_pairs={{0,1},{1,0},{2,3},{3,2},{4,5},{5,4},{6,7},{7,6},{8,9},{9,8},{10,11... | collective-permute-start | bytes 1179656 | tf_op jit(solution)/shard_map/ppermute | solution.py:39
  80.6 9.8 %collective-permute-start.17 = (f32[2,96,512]{2,1,0:T(8,128)S(1)}, f32[2,96,512]{2,1,0:T(8,128)S(1)}, u32[]{:S(2)}, u32[]{:S(2)}) collective-permute-start(f32[2,96,512]{2,1,0:T(8,128)S(1)} %paired.7), channel_id=1, source_target_pairs={{0,32},{1,225},{32,64},{33,1},{64,96},{65,33},{96,128},{97,65},{12... | collective-permute-start | bytes 1179656 | tf_op jit(solution)/shard_map/ppermute | solution.py:43
  85.7 13.9 %collective-permute-start.14 = (f32[4,96,512]{2,1,0:T(8,128)S(1)}, f32[4,96,512]{2,1,0:T(8,128)S(1)}, u32[]{:S(2)}, u32[]{:S(2)}) collective-permute-start(f32[4,96,512]{2,1,0:T(8,128)S(1)} %taken.7), channel_id=1, source_target_pairs={{0,1},{1,0},{2,3},{3,2},{4,5},{5,4},{6,7},{7,6},{8,9},{9,8},{10,11... | collective-permute-start | bytes 2359304 | tf_op jit(solution)/shard_map/ppermute | solution.py:39
  91.5 9.7 %collective-permute-start.18 = (f32[2,96,512]{2,1,0:T(8,128)S(1)}, f32[2,96,512]{2,1,0:T(8,128)S(1)}, u32[]{:S(2)}, u32[]{:S(2)}) collective-permute-start(f32[2,96,512]{2,1,0:T(8,128)S(1)} %paired.8), channel_id=1, source_target_pairs={{0,32},{1,225},{32,64},{33,1},{64,96},{65,33},{96,128},{97,65},{12... | collective-permute-start | bytes 1179656 | tf_op jit(solution)/shard_map/ppermute | solution.py:43
  97.6 9.7 %collective-permute-start.21 = (f32[2,96,512]{2,1,0:T(8,128)S(1)}, f32[2,96,512]{2,1,0:T(8,128)S(1)}, u32[]{:S(2)}, u32[]{:S(2)}) collective-permute-start(f32[2,96,512]{2,1,0:T(8,128)S(1)} %paired.11), channel_id=1, source_target_pairs={{0,32},{1,225},{32,64},{33,1},{64,96},{65,33},{96,128},{97,65},{12... | collective-permute-start | bytes 1179656 | tf_op jit(solution)/shard_map/ppermute | solution.py:43
  102.2 9.7 %collective-permute-start.19 = (f32[2,96,512]{2,1,0:T(8,128)S(1)}, f32[2,96,512]{2,1,0:T(8,128)S(1)}, u32[]{:S(2)}, u32[]{:S(2)}) collective-permute-start(f32[2,96,512]{2,1,0:T(8,128)S(1)} %paired.9), channel_id=1, source_target_pairs={{0,32},{1,225},{32,64},{33,1},{64,96},{65,33},{96,128},{97,65},{12... | collective-permute-start | bytes 1179656 | tf_op jit(solution)/shard_map/ppermute | solution.py:43
  108.3 11.9 %collective-permute-start.22 = (f32[2,96,512]{2,1,0:T(8,128)S(1)}, f32[2,96,512]{2,1,0:T(8,128)S(1)}, u32[]{:S(2)}, u32[]{:S(2)}) collective-permute-start(f32[2,96,512]{2,1,0:T(8,128)S(1)} %paired.12), channel_id=1, source_target_pairs={{0,32},{1,225},{32,64},{33,1},{64,96},{65,33},{96,128},{97,65},{12... | collective-permute-start | bytes 1179656 | tf_op jit(solution)/shard_map/ppermute | solution.py:43
  113.0 23.4 %copy-start = (s32[256]{0:T(256)S(1)}, s32[256]{0:T(256)}, u32[]{:S(2)}) copy-start(s32[256]{0:T(256)} %accepted.1) | copy-start | bytes 3076
  113.0 14.6 %collective-permute-start.20 = (f32[2,96,512]{2,1,0:T(8,128)S(1)}, f32[2,96,512]{2,1,0:T(8,128)S(1)}, u32[]{:S(2)}, u32[]{:S(2)}) collective-permute-start(f32[2,96,512]{2,1,0:T(8,128)S(1)} %paired.10), channel_id=1, source_target_pairs={{0,288},{1,481},{32,320},{33,257},{64,352},{65,289},{96,384},{97,3... | collective-permute-start | bytes 1179656 | tf_op jit(solution)/shard_map/ppermute | solution.py:323
  121.3 30.0 %copy-start.2 = (f32[512]{0:T(512)S(1)}, f32[512]{0:T(512)}, u32[]{:S(2)}) copy-start(f32[512]{0:T(512)} %param.15) | copy-start | bytes 6148
  121.3 9.3 %collective-permute-start.23 = (f32[2,96,512]{2,1,0:T(8,128)S(1)}, f32[2,96,512]{2,1,0:T(8,128)S(1)}, u32[]{:S(2)}, u32[]{:S(2)}) collective-permute-start(f32[2,96,512]{2,1,0:T(8,128)S(1)} %paired.13), channel_id=1, source_target_pairs={{0,32},{1,225},{32,64},{33,1},{64,96},{65,33},{96,128},{97,65},{12... | collective-permute-start | bytes 1179656 | tf_op jit(solution)/shard_map/ppermute | solution.py:43
  124.2 13.4 %collective-permute-start.13 = (f32[96,512]{1,0:T(8,128)S(1)}, f32[96,512]{1,0:T(8,128)S(1)}, u32[]{:S(2)}, u32[]{:S(2)}) collective-permute-start(f32[96,512]{1,0:T(8,128)S(1)} %bitcast.28), channel_id=1, source_target_pairs={{0,256},{256,0},{1,257},{257,1},{2,258},{258,2},{3,259},{259,3},{4... | collective-permute-start | bytes 589832 | tf_op jit(solution)/shard_map/ppermute | solution.py:310
  130.6 7.0 %collective-permute-start.24 = (f32[96,512]{1,0:T(8,128)S(1)}, f32[96,512]{1,0:T(8,128)}, u32[]{:S(2)}, u32[]{:S(2)}) collective-permute-start(f32[96,512]{1,0:T(8,128)S(1)} %fusion), channel_id=1, source_target_pairs={{0,1},{1,0},{2,3},{3,2},{4,5},{5,4},{6,7},{7,6},{8,9},{9,8},{10,11... | collective-permute-start | bytes 589832 | tf_op jit(solution)/shard_map/ppermute | solution.py:39
  139.4 11.8 %all-to-all-start = ((f32[32,1,96]{2,1,0:T(1,128)}), f32[32,1,96]{2,1,0:T(1,128)S(1)}, u32[]{:S(2)}, u32[]{:S(2)}) async-start(f32[32,1,96]{2,1,0:T(1,128)} %broadcast_in_dim.45), calls=%async_computation | async-start | bytes 32768 | tf_op jit(solution)/shard_map/all_to_all | solution.py:331
